TPU v7x, 512 devices: a whole 4x4x16 slice. The times are simulated.
512 devices in a mesh: ctx: 128 (over z, y, core), head: 4 (over x).
Axes of the slice: x: 4, y: 4, z: 16, core: 2. Of those that a mesh axis runs over, the one named last changes fastest.
Arguments:
- queries: bfloat16 [16384, 32, 128], P('ctx', 'head'), may hold values from -22 to 22
- key_states: bfloat16 [16384, 8, 128], P('ctx'), may hold values from -22 to 22
- value_states: bfloat16 [16384, 8, 128], P('ctx'), may hold values from -5 to 5
- grad_out: bfloat16 [16384, 32, 128], P('ctx', 'head'), may hold values from -5 to 5
- selected: int32 [256, 32, 3], P(None, 'head'), may hold values from 0 to 255, as said below
Outputs:
- attention_out: bfloat16 [16384, 32, 128], P('ctx', 'head')
- query_grad: bfloat16 [16384, 32, 128], P('ctx', 'head')
- key_grad: bfloat16 [16384, 8, 128], P('ctx', 'head')
- value_grad: bfloat16 [16384, 8, 128], P('ctx', 'head')
Inputs may be any that keep to these rules, and one draw needn't show every extreme that they name: `selected`: for every ctx shard s and head group g, the 48 entries of blocks s * 2 to (s + 1) * 2 - 1 and the group's 8 heads name only blocks of other shards, no shard more than 1 times and some shard exactly 1 times; the 3 entries of one block and head name blocks of different shards.
All inputs are finite; a program needn't handle non-finite values.
Results may differ from a plain program's by a relative error of at most 0.03.
Values may be sent and summed in bfloat16 or wider, within the bound.
A program may use at most 64 MiB of HBM per device.

v0:
```python
import jax
import jax.numpy as jnp
import numpy as np
from jax import lax
from jax.sharding import PartitionSpec as P

BLOCK = 64


def in_one_piece(arrays, axis, split_dim, concat_dim, along):
    both = jnp.concatenate(arrays, axis=along)
    whole, at, done = (
        lax.all_to_all(both, axis, split_axis=split_dim, concat_axis=concat_dim, tiled=True),
        0,
        [],
    )
    for a in arrays:
        done.append(lax.slice_in_dim(whole, at, at + a.shape[along], axis=along))
        at += a.shape[along]
    return tuple(done)


def split_up(value, dim, length):
    dims = value.shape
    tiles = value.reshape(*dims[:dim], length, dims[dim] // length, *dims[dim + 1 :])
    return jnp.moveaxis(tiles, dim, 0)


def sent_and_summed(value, axis, dim):
    length = lax.axis_size(axis)
    tiles = lax.all_to_all(split_up(value, dim, length), axis, 0, 0, tiled=True)
    return jnp.sum(tiles.astype(jnp.float32), axis=0)


def sent_together(arrays, axis, dim, along):
    ends, at = ([], 0)
    for a in arrays[:-1]:
        at += a.shape[along]
        ends.append(at)
    both = jnp.concatenate(arrays, axis=along)
    return tuple(jnp.split(sent_and_summed(both, axis, dim), ends, axis=along))


def to_units(stacked, blocks):
    row_count, head_count, feature = stacked.shape
    length = row_count // blocks
    return (
        stacked.reshape(blocks, length, head_count, feature)
        .transpose(0, 2, 1, 3)
        .reshape(blocks * head_count, length, feature)
    )


def from_units(stacked, blocks, head_count):
    unit_count, length, feature = stacked.shape
    return (
        stacked.reshape(blocks, head_count, length, feature)
        .transpose(0, 2, 1, 3)
        .reshape(blocks * length, head_count, feature)
    )


def partial_forward(query_units, key_sets, value_sets, factor):
    scores = (
        jnp.einsum("nqh,ntkh->ntqk", query_units, key_sets, preferred_element_type=jnp.float32)
        * factor
    )
    block_max = jnp.max(scores, axis=-1)
    exp_scores = jnp.exp(scores - block_max[..., None])
    block_sum = jnp.sum(exp_scores, axis=-1)
    block_out = jnp.einsum(
        "ntqk,ntkh->ntqh",
        exp_scores.astype(jnp.bfloat16),
        value_sets,
        preferred_element_type=jnp.float32,
    ).astype(jnp.bfloat16)
    return (block_max, block_sum, block_out)


def partial_backward(query_units, key_sets, value_sets, grad_units, log_total, row_delta, factor):
    scores = (
        jnp.einsum("nqh,ntkh->ntqk", query_units, key_sets, preferred_element_type=jnp.float32)
        * factor
    )
    probability = jnp.exp(scores - log_total[:, None, :, None])
    grad_prob = jnp.einsum(
        "nqh,ntkh->ntqk", grad_units, value_sets, preferred_element_type=jnp.float32
    )
    grad_scores = (probability * (grad_prob - row_delta[:, None, :, None])).astype(jnp.bfloat16)
    query_terms = (
        jnp.einsum("ntqk,ntkh->ntqh", grad_scores, key_sets, preferred_element_type=jnp.float32)
        * factor
    ).astype(jnp.bfloat16)
    key_terms = (
        jnp.einsum("ntqk,nqh->ntkh", grad_scores, query_units, preferred_element_type=jnp.float32)
        * factor
    ).astype(jnp.bfloat16)
    value_terms = jnp.einsum(
        "ntqk,nqh->ntkh",
        probability.astype(jnp.bfloat16),
        grad_units,
        preferred_element_type=jnp.float32,
    ).astype(jnp.bfloat16)
    return (query_terms, key_terms, value_terms)


def local(queries, key_states, value_states, grad_out, selected):
    rows_dev, query_heads, head_size = queries.shape
    kv_heads = key_states.shape[1]
    blocks_dev = rows_dev // BLOCK
    top_count = selected.shape[2]
    shard_count = lax.axis_size("ctx")
    shard_index = lax.axis_index("ctx")
    factor = head_size ** (-0.5)
    repeats = query_heads // kv_heads
    home_units = blocks_dev * query_heads
    request_count = home_units * top_count
    capacity = (request_count + shard_count - 2) // (shard_count - 1)
    slot_count = shard_count * capacity
    kv_units = blocks_dev * kv_heads
    query_units = to_units(queries, blocks_dev)
    grad_units = to_units(grad_out, blocks_dev)
    key_units = to_units(key_states, blocks_dev)
    value_units = to_units(value_states, blocks_dev)

    def own_sets(unit_array):
        shaped = unit_array.reshape(blocks_dev, 1, kv_heads, BLOCK, head_size)
        return shaped.reshape(home_units, 1, BLOCK, head_size)

    own_keys = own_sets(key_units)
    own_values = own_sets(value_units)
    my_lists = lax.dynamic_slice_in_dim(selected, shard_index * blocks_dev, blocks_dev, 0).reshape(
        request_count
    )
    target = my_lists // blocks_dev
    target_hits = (target[:, None] == jnp.arange(shard_count, dtype=jnp.int32)[None, :]).astype(
        jnp.int32
    )
    earlier = jnp.cumsum(target_hits, axis=0) - target_hits
    position = target * capacity + jnp.sum(earlier * target_hits, axis=1)
    all_lists = selected.reshape(shard_count, request_count)
    owner_hits = (all_lists // blocks_dev == shard_index).astype(jnp.int32)
    owner_rank = jnp.cumsum(owner_hits, axis=1) - owner_hits
    head_of_request = jnp.asarray(
        np.arange(request_count) // top_count % query_heads % kv_heads, dtype=jnp.int32
    )
    unit_of_request = all_lists % blocks_dev * kv_heads + head_of_request[None, :]
    slot_match = (
        owner_rank[:, None, :] == jnp.arange(capacity, dtype=jnp.int32)[None, :, None]
    ).astype(jnp.int32)
    picked = owner_hits[:, None, :] * slot_match
    slot_units = jnp.sum(picked * unit_of_request[:, None, :], axis=2).reshape(slot_count)
    slot_filled = jnp.sum(picked, axis=2).reshape(slot_count)
    collect_matrix = (
        (slot_units[None, :] == jnp.arange(kv_units, dtype=jnp.int32)[:, None])
        & (slot_filled[None, :] > 0)
    ).astype(jnp.bfloat16)
    own_max, own_sum, own_out = partial_forward(query_units, own_keys, own_values, factor)
    send_keys = jnp.take(key_units, slot_units, axis=0)
    send_values = jnp.take(value_units, slot_units, axis=0)
    recv_keys, recv_values = in_one_piece((send_keys, send_values), "ctx", 0, 0, 1)
    fetched_keys = jnp.take(recv_keys, position, axis=0).reshape(
        home_units, top_count, BLOCK, head_size
    )
    fetched_values = jnp.take(recv_values, position, axis=0).reshape(
        home_units, top_count, BLOCK, head_size
    )
    far_max, far_sum, far_out = partial_forward(query_units, fetched_keys, fetched_values, factor)
    block_max = jnp.concatenate([own_max, far_max], axis=1)
    block_sum = jnp.concatenate([own_sum, far_sum], axis=1)
    block_out = jnp.concatenate([own_out, far_out], axis=1)
    overall_max = jnp.max(block_max, axis=1)
    weight = jnp.exp(block_max - overall_max[:, None])
    denominator = jnp.sum(weight * block_sum, axis=1)
    attended = (
        jnp.sum(weight[..., None] * block_out.astype(jnp.float32), axis=1) / denominator[..., None]
    ).astype(jnp.bfloat16)
    log_total = overall_max + jnp.log(denominator)
    row_delta = jnp.sum(grad_units.astype(jnp.float32) * attended.astype(jnp.float32), axis=-1)
    own_query, own_key, own_value = partial_backward(
        query_units, own_keys, own_values, grad_units, log_total, row_delta, factor
    )
    own_key_sum = jnp.sum(
        own_key.astype(jnp.float32).reshape(blocks_dev, repeats, kv_heads, BLOCK, head_size), axis=1
    ).reshape(kv_units, BLOCK, head_size)
    own_value_sum = jnp.sum(
        own_value.astype(jnp.float32).reshape(blocks_dev, repeats, kv_heads, BLOCK, head_size),
        axis=1,
    ).reshape(kv_units, BLOCK, head_size)
    far_query, far_key, far_value = partial_backward(
        query_units, fetched_keys, fetched_values, grad_units, log_total, row_delta, factor
    )
    empty_slots = jnp.zeros((slot_count, BLOCK, head_size), jnp.bfloat16)
    send_key_terms = empty_slots.at[position].set(far_key.reshape(request_count, BLOCK, head_size))
    send_value_terms = empty_slots.at[position].set(
        far_value.reshape(request_count, BLOCK, head_size)
    )
    recv_key_terms, recv_value_terms = (
        lax.all_to_all(send_key_terms, "ctx", split_axis=0, concat_axis=0, tiled=True),
        lax.all_to_all(send_value_terms, "ctx", split_axis=0, concat_axis=0, tiled=True),
    )
    far_query_sum = jnp.sum(far_query.astype(jnp.float32), axis=1)
    query_total = (own_query[:, 0].astype(jnp.float32) + far_query_sum).astype(jnp.bfloat16)
    remote_keys = jnp.dot(
        collect_matrix,
        recv_key_terms.reshape(slot_count, BLOCK * head_size),
        preferred_element_type=jnp.float32,
    )
    remote_values = jnp.dot(
        collect_matrix,
        recv_value_terms.reshape(slot_count, BLOCK * head_size),
        preferred_element_type=jnp.float32,
    )
    key_total = own_key_sum + remote_keys.reshape(kv_units, BLOCK, head_size)
    value_total = own_value_sum + remote_values.reshape(kv_units, BLOCK, head_size)
    key_full = from_units(key_total, blocks_dev, kv_heads)
    value_full = from_units(value_total, blocks_dev, kv_heads)
    key_part, value_part = sent_together(
        (key_full.astype(jnp.bfloat16), value_full.astype(jnp.bfloat16)), "head", 1, 0
    )
    attention_out = from_units(attended, blocks_dev, query_heads)
    query_grad = from_units(query_total, blocks_dev, query_heads)
    return (
        attention_out,
        query_grad,
        key_part.astype(jnp.bfloat16),
        value_part.astype(jnp.bfloat16),
    )


def solution(mesh):
    placed = (
        P("ctx", "head", None),
        P("ctx", None, None),
        P("ctx", None, None),
        P("ctx", "head", None),
        P(None, "head", None),
    )
    return jax.shard_map(
        local,
        mesh=mesh,
        in_specs=placed,
        out_specs=(
            P("ctx", "head", None),
            P("ctx", "head", None),
            P("ctx", "head", None),
            P("ctx", "head", None),
        ),
        check_vma=False,
    )
```

profile of v0, /device:TPU:6, one launch (start us, length us, event | category | flops | bytes accessed | tf_op | source)
XLA Modules:
  0.0 475.1 jit_solution(7638517871893264330)
XLA Ops:
  0.6 1.2 copy.122
  1.9 0.5 reshape.329
  2.6 0.6 reduce_window_sum.25
  3.2 0.4 copy.128
  4.3 1.0 gather_fusion
  5.3 2.2 gather_fusion.1
  7.5 2.0 broadcast_select_fusion.1
  9.5 2.4 pad_maximum_fusion
  11.9 20.6 %all-to-all-start = ((bf16[128,128,128]{2,1,0:T(8,128)(2,1)}), bf16[128,128,128]{2,1,0:T(8,128)(2,1)}, u32[]{:S(2)}, u32[]{:S(2)}) async-start(bf16[128,128,128]{2,1,0:T(8,128)(2,1)} %pad_maximum_fusion), calls=%async_computation | async-start | bytes 8388608 | tf_op jit(solution)/shard_map/all_to_all | solution.py:13
  33.2 0.8 copy.136
  34.6 184.4 %all-to-all-done = bf16[128,128,128]{2,1,0:T(8,128)(2,1)} async-done(((bf16[128,128,128]{2,1,0:T(8,128)(2,1)}), bf16[128,128,128]{2,1,0:T(8,128)(2,1)}, u32[]{:S(2)}, u32[]{:S(2)}) %all-to-all-start) | async-done | bytes 4194336 | tf_op jit(solution)/shard_map/all_to_all | solution.py:13
  219.0 4.5 fusion.68
  223.5 3.1 gather_fusion.3
  226.7 1.6 gather_fusion.2
  228.2 1.6 broadcast_select_fusion.2
  229.9 0.4 bitcast_reduce_fusion.1
  230.3 0.5 fusion.8
  231.0 1.2 convolution_convert_fusion.1
  232.3 1.8 broadcast_in_dim.17.clone
  234.1 6.9 %scatter_fusion.1 = bf16[128,64,128]{2,1,0:T(8,128)(2,1)} fusion(bf16[128,64,128]{2,1,0:T(8,128)(2,1)} %broadcast_in_dim.17.clone, s32[48]{0:T(128)S(1)} %fusion.65, bf16[48,64,128]{2,1,0:T(8,128)(2,1)} %bitcast.178), kind=kCustom, calls=%fused_computation.5 | custom fusion | bytes 2359488 | tf_op jit(solution)/shard_map/scatter | solution.py:195
  241.0 10.8 %all-to-all-start.2 = ((bf16[128,64,128]{2,1,0:T(8,128)(2,1)}), bf16[128,64,128]{2,1,0:T(8,128)(2,1)}, u32[]{:S(2)}, u32[]{:S(2)}) async-start(bf16[128,64,128]{2,1,0:T(8,128)(2,1)} %scatter_fusion.1), calls=%async_computation.2 | async-start | bytes 4194304 | tf_op jit(solution)/shard_map/all_to_all | solution.py:200
  251.9 0.3 fusion.26
  252.2 0.4 convolution_convert_fusion
  252.6 0.7 multiply_reduce_fusion
  253.4 0.9 multiply_reduce_fusion.1
  254.3 0.4 fusion.4
  254.8 0.9 copy-done
  255.6 0.3 multiply_convert_fusion
  256.0 1.9 broadcast_in_dim.17.clone.1
  257.8 6.2 %scatter_fusion = bf16[128,64,128]{2,1,0:T(8,128)(2,1)} fusion(bf16[128,64,128]{2,1,0:T(8,128)(2,1)} %broadcast_in_dim.17.clone.1, s32[48]{0:T(128)S(1)} %fusion.65, bf16[48,64,128]{2,1,0:T(8,128)(2,1)S(1)} %bitcast.177), kind=kCustom, calls=%fused_computation.4 | custom fusion | bytes 2359488 | tf_op jit(solution)/shard_map/scatter | solution.py:194
  264.1 85.4 %all-to-all-done.2 = bf16[128,64,128]{2,1,0:T(8,128)(2,1)} async-done(((bf16[128,64,128]{2,1,0:T(8,128)(2,1)}), bf16[128,64,128]{2,1,0:T(8,128)(2,1)}, u32[]{:S(2)}, u32[]{:S(2)}) %all-to-all-start.2) | async-done | bytes 2097184 | tf_op jit(solution)/shard_map/all_to_all | solution.py:200
  349.4 8.8 %all-to-all-start.1 = ((bf16[128,64,128]{2,1,0:T(8,128)(2,1)}), bf16[128,64,128]{2,1,0:T(8,128)(2,1)S(1)}, u32[]{:S(2)}, u32[]{:S(2)}) async-start(bf16[128,64,128]{2,1,0:T(8,128)(2,1)} %scatter_fusion), calls=%async_computation.1 | async-start | bytes 4194304 | tf_op jit(solution)/shard_map/all_to_all | solution.py:199
  358.5 1.8 copy.135
  360.3 1.0 fusion.27
  361.3 4.2 copy.156
  365.5 2.2 fusion
  367.7 0.3 fusion.17
  368.1 88.4 %all-to-all-done.1 = bf16[128,64,128]{2,1,0:T(8,128)(2,1)S(1)} async-done(((bf16[128,64,128]{2,1,0:T(8,128)(2,1)}), bf16[128,64,128]{2,1,0:T(8,128)(2,1)S(1)}, u32[]{:S(2)}, u32[]{:S(2)}) %all-to-all-start.1) | async-done | bytes 2097184 | tf_op jit(solution)/shard_map/all_to_all | solution.py:199
  456.4 2.9 copy.155
  459.3 2.3 fusion.2
  461.7 0.3 fusion.25
  462.0 0.8 maximum_bitcast_fusion
  462.8 4.8 %all-to-all-start.3 = ((bf16[4,256,2,128]{3,1,2,0:T(8,128)(2,1)}), bf16[4,256,2,128]{3,1,2,0:T(8,128)(2,1)S(1)}, u32[]{:S(2)}, u32[]{:S(2)}) async-start(bf16[4,256,2,128]{3,1,2,0:T(8,128)(2,1)} %maximum_bitcast_fusion), calls=%async_computation.3 | async-start | bytes 1048576 | tf_op jit(solution)/shard_map/all_to_all | solution.py:31
  467.6 0.4 convert_reduce_fusion
  468.3 0.9 copy.139
  469.2 4.4 all-to-all-done.3
  473.7 0.7 copy.147
  474.4 0.7 copy.148
  (76 shorter events, 3.1 us)
Async XLA Ops:
  0.6 3.0 copy-start.18
  1.8 2.0 copy-start.17
  1.8 2.4 copy-start.14
  2.4 1.9 copy-start.15
  11.9 21.2 %copy-start.16 = (bf16[128,8,128]{2,1,0:T(8,128)(2,1)S(1)}, bf16[128,8,128]{2,1,0:T(8,128)(2,1)}, u32[]{:S(2)}) copy-start(bf16[128,8,128]{2,1,0:T(8,128)(2,1)} %param.10) | copy-start | bytes 786436
  11.9 21.3 %copy-start.12 = (bf16[128,8,128]{2,1,0:T(8,128)(2,1)S(1)}, bf16[128,8,128]{2,1,0:T(8,128)(2,1)}, u32[]{:S(2)}) copy-start(bf16[128,8,128]{2,1,0:T(8,128)(2,1)} %param.13) | copy-start | bytes 786436
  11.9 207.1 %all-to-all-start = ((bf16[128,128,128]{2,1,0:T(8,128)(2,1)}), bf16[128,128,128]{2,1,0:T(8,128)(2,1)}, u32[]{:S(2)}, u32[]{:S(2)}) async-start(bf16[128,128,128]{2,1,0:T(8,128)(2,1)} %pad_maximum_fusion), calls=%async_computation | async-start | bytes 8388608 | tf_op jit(solution)/shard_map/all_to_all | solution.py:13
  33.2 190.4 %copy-start.4 = (bf16[2,8,64,128]{3,2,1,0:T(8,128)(2,1)}, bf16[2,8,64,128]{3,2,1,0:T(8,128)(2,1)S(1)}, u32[]{:S(2)}) copy-start(bf16[2,8,64,128]{3,2,1,0:T(8,128)(2,1)S(1)} %copy.120) | copy-start | bytes 786436
  228.2 1.6 copy-start.5
  229.9 0.9 copy-start.2
  229.9 1.2 copy-start.8
  241.0 108.4 %all-to-all-start.2 = ((bf16[128,64,128]{2,1,0:T(8,128)(2,1)}), bf16[128,64,128]{2,1,0:T(8,128)(2,1)}, u32[]{:S(2)}, u32[]{:S(2)}) async-start(bf16[128,64,128]{2,1,0:T(8,128)(2,1)} %scatter_fusion.1), calls=%async_computation.2 | async-start | bytes 4194304 | tf_op jit(solution)/shard_map/all_to_all | solution.py:200
  252.2 1.2 copy-start.13
  252.6 1.7 copy-start.9
  254.3 1.3 copy-start.6
  254.8 0.9 copy-start
  264.1 96.3 %copy-start.10 = (bf16[2,64,8,128]{3,1,2,0:T(8,128)(2,1)S(1)}, bf16[2,64,8,128]{3,1,2,0:T(8,128)(2,1)}, u32[]{:S(2)}) copy-start(bf16[2,64,8,128]{3,1,2,0:T(8,128)(2,1)} %copy.136) | copy-start | bytes 786436
  349.4 107.0 %all-to-all-start.1 = ((bf16[128,64,128]{2,1,0:T(8,128)(2,1)}), bf16[128,64,128]{2,1,0:T(8,128)(2,1)S(1)}, u32[]{:S(2)}, u32[]{:S(2)}) async-start(bf16[128,64,128]{2,1,0:T(8,128)(2,1)} %scatter_fusion), calls=%async_computation.1 | async-start | bytes 4194304 | tf_op jit(solution)/shard_map/all_to_all | solution.py:199
  459.3 2.3 copy-start.7
  459.3 2.3 copy-start.11
  461.6 6.0 %copy-start.1 = (bf16[16,3,64,64]{2,3,1,0:T(8,128)(2,1)S(1)}, bf16[16,3,64,64]{2,3,1,0:T(8,128)(2,1)}, u32[]{:S(2)}) copy-start(bf16[16,3,64,64]{2,3,1,0:T(8,128)(2,1)} %copy-done) | copy-start | bytes 1179652
  461.7 5.9 %copy-start.3 = (bf16[48,64,128]{2,1,0:T(8,128)(2,1)S(1)}, bf16[48,64,128]{2,1,0:T(8,128)(2,1)}, u32[]{:S(2)}) copy-start(bf16[48,64,128]{2,1,0:T(8,128)(2,1)} %copy-done.2) | copy-start | bytes 2359300
  462.8 10.8 %all-to-all-start.3 = ((bf16[4,256,2,128]{3,1,2,0:T(8,128)(2,1)}), bf16[4,256,2,128]{3,1,2,0:T(8,128)(2,1)S(1)}, u32[]{:S(2)}, u32[]{:S(2)}) async-start(bf16[4,256,2,128]{3,1,2,0:T(8,128)(2,1)} %maximum_bitcast_fusion), calls=%async_computation.3 | async-start | bytes 1048576 | tf_op jit(solution)/shard_map/all_to_all | solution.py:31
where the time goes:
time: 480 us; the launch traced here: 475 us
  waiting for transfers between devices  363 us (76%)
  local copies, waits for them, and re-layouts  46.2 us (10%)
  starting transfers between devices  45 us (9%)
  matrix products  10.2 us (2%)
  other arithmetic  10.1 us (2%)
    all_to_all x1, waiting for transfers between devices, in_one_piece(): lax.all_to_all(both, axis, split_axis=split_dim, concat_axis=concat_dim,...  184 us
    all_to_all x1, waiting for transfers between devices, local(): lax.all_to_all(send_key_terms, 'ctx', split_axis=0, concat_axis=0, tiled=...  88.4 us
    all_to_all x1, waiting for transfers between devices, local(): lax.all_to_all(send_value_terms, 'ctx', split_axis=0, concat_axis=0, tile...  85.4 us
    all_to_all x1, starting transfers between devices, in_one_piece(): lax.all_to_all(both, axis, split_axis=split_dim, concat_axis=concat_dim,...  20.6 us
    scatter x2, local copies, waits for them, and re-layouts, local(): empty_slots.at[position]  13.2 us
    all_to_all x1, starting transfers between devices, local(): lax.all_to_all(send_value_terms, 'ctx', split_axis=0, concat_axis=0, tile...  10.8 us
  transfers between devices with their start and end apart: 4, of which 4 were waited for; matrix products, arithmetic and copies ran while one was open for 5% of the time, Pallas kernels for 0%

commit v1 on v0

v1 whole, which is shorter than its diff:
```python
import functools

import jax
import jax.numpy as jnp
from jax import lax
from jax.experimental import pallas as pl
from jax.experimental.pallas import tpu as pltpu
from jax.sharding import PartitionSpec as P

BLOCK = 64
HEAD = 128
SIDE = 4
PLANE = SIDE * SIDE
MESH = pl.DeviceIdType.MESH
ANY = pl.BlockSpec(memory_space=pl.ANY)
VMEM = pl.BlockSpec(memory_space=pltpu.VMEM)
SMEM = pl.BlockSpec(memory_space=pltpu.SMEM)


def place():
    ctx = lax.axis_index("ctx")
    x = lax.axis_index("head")
    return x, (ctx // 2) % SIDE, ctx // (2 * SIDE), ctx % 2


def ctx_of(z, y, core):
    return (z * SIDE + y) * 2 + core


def unit_of(x, y):
    return (y % 2) * 8 + 2 * x + y // 2


def greet(planes, x, y, z, core):
    barrier = pltpu.get_barrier_semaphore()

    def one(k, carry):
        t = (x * SIDE + y + k) % PLANE
        pl.semaphore_signal(
            barrier, inc=1, device_id=(ctx_of(z, t % SIDE, core), t // SIDE), device_id_type=MESH
        )
        return carry

    for other in (
        ctx_of((z + 1) % planes, y, core),
        ctx_of((z + planes - 1) % planes, y, core),
        ctx_of(z, y, 1 - core),
    ):
        pl.semaphore_signal(barrier, inc=1, device_id=(other, x), device_id_type=MESH)
    lax.fori_loop(1, PLANE, one, 0)
    pl.semaphore_wait(barrier, PLANE + 2)


def remote(src, dst, send, recv, ctx, x):
    return pltpu.make_async_remote_copy(
        src_ref=src, dst_ref=dst, send_sem=send, recv_sem=recv, device_id=(ctx, x), device_id_type=MESH
    )


def bring(
    planes,
    qd,
    sel,
    kv,
    qd_out,
    sel_out,
    store,
    near_send,
    near_recv,
    q_send,
    q_recv,
    i_send,
    i_recv,
    ring_send,
    ring_recv,
    pair_send,
    pair_recv,
    own_sem,
):
    x, y, z, core = place()
    half_way = planes // 2
    greet(planes, x, y, z, core)

    def near(d):
        to = (y + d) % SIDE
        return remote(
            kv.at[to // 2],
            store.at[pl.ds(z * 16 + core * 8 + y * 2, 2)],
            near_send.at[d - 1],
            near_recv.at[d - 1],
            ctx_of(z, to, core),
            x,
        )

    def query(k):
        t = (x * SIDE + y + k) % PLANE
        return remote(
            qd.at[unit_of(t // SIDE, t % SIDE)],
            qd_out.at[x * SIDE + y],
            q_send.at[k - 1],
            q_recv.at[k - 1],
            ctx_of(z, t % SIDE, core),
            t // SIDE,
        )

    def index(k):
        t = (x * SIDE + y + k) % PLANE
        return remote(
            sel.at[unit_of(t // SIDE, t % SIDE)],
            sel_out.at[x * SIDE + y],
            i_send.at[k - 1],
            i_recv.at[k - 1],
            ctx_of(z, t % SIDE, core),
            t // SIDE,
        )

    def rows(origin, half):
        return store.at[pl.ds(((origin + planes) % planes) * 16 + core * 8 + half * 4, 4)]

    def origin_of(d, s):
        return z - s if d == 0 else z + s

    def hop(d, s, half):
        to = (z + 1) % planes if d == 0 else (z + planes - 1) % planes
        piece = rows(origin_of(d, s - 1), half)
        return remote(
            piece,
            piece,
            ring_send.at[d, s - 1, half],
            ring_recv.at[d, s - 1, half],
            ctx_of(to, y, core),
            x,
        )

    def arrived(d, s, half):
        piece = rows(origin_of(d, s), half)
        return remote(
            piece,
            piece,
            ring_send.at[d, s - 1, half],
            ring_recv.at[d, s - 1, half],
            ctx_of(z, y, 1 - core),
            x,
        )

    def share(d, s, half):
        piece = rows(origin_of(d, s), half)
        return remote(
            piece,
            piece,
            pair_send.at[d, s, half],
            pair_recv.at[d, s, half],
            ctx_of(z, y, 1 - core),
            x,
        )

    def shared(d, s, half):
        piece = store.at[
            pl.ds(((origin_of(d, s) + planes) % planes) * 16 + (1 - core) * 8 + half * 4, 4)
        ]
        return remote(
            piece,
            piece,
            pair_send.at[d, s, half],
            pair_recv.at[d, s, half],
            ctx_of(z, y, 1 - core),
            x,
        )

    for d in range(1, SIDE):
        near(d).start()
    mine = (
        pltpu.make_async_copy(
            kv.at[y // 2], store.at[pl.ds(z * 16 + core * 8 + y * 2, 2)], own_sem.at[0]
        ),
        pltpu.make_async_copy(qd.at[unit_of(x, y)], qd_out.at[x * SIDE + y], own_sem.at[1]),
        pltpu.make_async_copy(sel.at[unit_of(x, y)], sel_out.at[x * SIDE + y], own_sem.at[2]),
    )
    for copy in mine:
        copy.start()

    def send_query(k, carry):
        query(k).start()
        index(k).start()
        return carry

    lax.fori_loop(1, PLANE, send_query, 0)
    mine[0].wait()
    for d in range(1, SIDE):
        near(d).wait_recv()

    for half in range(2):
        for d in range(2):
            hop(d, 1, half).start()
        share(0, 0, half).start()

    def step(s, carry):
        for half in range(2):
            for d in range(2):
                arrived(d, s - 1, half).wait_recv()
                hop(d, s, half).start()
                share(d, s - 1, half).start()
        return carry

    lax.fori_loop(2, half_way, step, 0)
    for half in range(2):
        for d in range(2):
            arrived(d, half_way - 1, half).wait_recv()
            if half == d:
                hop(d, half_way, half).start()
            share(d, half_way - 1, half).start()
    for d in range(2):
        arrived(d, half_way, d).wait_recv()
        share(d, half_way, d).start()

    for half in range(2):
        shared(0, 0, half).wait_recv()
        share(0, 0, half).wait_send()

    def finish(s, carry):
        for half in range(2):
            for d in range(2):
                hop(d, s, half).wait_send()
                shared(d, s, half).wait_recv()
                share(d, s, half).wait_send()
        return carry

    lax.fori_loop(1, half_way, finish, 0)
    for d in range(2):
        hop(d, half_way, d).wait_send()
        shared(d, half_way, d).wait_recv()
        share(d, half_way, d).wait_send()
        mine[d + 1].wait()
    for d in range(1, SIDE):
        near(d).wait_send()

    def finish_query(k, carry):
        query(k).wait()
        index(k).wait()
        return carry

    lax.fori_loop(1, PLANE, finish_query, 0)


def attend(sel, qd, store, od, acc_out, kv, acc, stage, load_sem, out_sem):
    x, y, z, core = place()
    parity = y % 2
    factor = HEAD**-0.5
    f32 = jnp.float32

    def row_of(u, t):
        if t == 0:
            return z * 16 + core * 8 + (u % SIDE) * 2 + parity
        n = sel[u, 0, t - 1]
        return (n // 16) * 16 + ((n // 2) % 2) * 8 + ((n // 4) % SIDE) * 2 + n % 2

    def fetch(u, carry):
        for t in range(4):
            pltpu.make_async_copy(store.at[row_of(u, t)], kv.at[u, t], load_sem.at[u]).start()
        return carry

    lax.fori_loop(0, PLANE, fetch, 0)

    def clear(i, carry):
        acc[pl.ds(i * 2, 2)] = jnp.zeros((2, 2, BLOCK, HEAD), f32)
        return carry

    lax.fori_loop(0, acc.shape[0] // 2, clear, 0)

    def one(u, carry):
        pltpu.make_async_copy(store.at[pl.ds(0, 4)], kv.at[u], load_sem.at[u]).wait()
        q = qd[u, 0]
        g = qd[u, 1]
        keys = kv[u, :, 0].reshape(4 * BLOCK, HEAD)
        values = kv[u, :, 1].reshape(4 * BLOCK, HEAD)
        nt = (((1,), (1,)), ((), ()))
        nn = (((1,), (0,)), ((), ()))
        tn = (((0,), (0,)), ((), ()))
        scores = lax.dot_general(q, keys, nt, preferred_element_type=f32) * factor
        top = jnp.max(scores, axis=1, keepdims=True)
        e = jnp.exp(scores - top)
        inverse = 1.0 / jnp.sum(e, axis=1, keepdims=True)
        prob = e * inverse
        prob_b = prob.astype(jnp.bfloat16)
        out = lax.dot_general(prob_b, values, nn, preferred_element_type=f32).astype(jnp.bfloat16)
        od[u, 0] = out
        delta = jnp.sum(g.astype(f32) * out.astype(f32), axis=1, keepdims=True)
        grad_prob = lax.dot_general(g, values, nt, preferred_element_type=f32)
        grad_scores = (prob * (grad_prob - delta)).astype(jnp.bfloat16)
        od[u, 1] = (
            lax.dot_general(grad_scores, keys, nn, preferred_element_type=f32) * factor
        ).astype(jnp.bfloat16)
        key_terms = lax.dot_general(grad_scores, q, tn, preferred_element_type=f32) * factor
        value_terms = lax.dot_general(prob_b, g, tn, preferred_element_type=f32)
        for t in range(4):
            row = row_of(u, t)
            part = slice(t * BLOCK, (t + 1) * BLOCK)
            acc[row, 0] += key_terms[part]
            acc[row, 1] += value_terms[part]
        return carry

    lax.fori_loop(0, PLANE, one, 0)

    pieces = stage.shape[0] // 16

    def leave(i):
        return pltpu.make_async_copy(
            stage.at[pl.ds(i * 16, 16)], acc_out.at[pl.ds(i * 16, 16)], out_sem.at[i]
        )

    def pack(i, carry):
        def four(k, c):
            at = pl.ds(i * 16 + k * 2, 2)
            stage[at] = acc[at].astype(jnp.bfloat16)
            return c

        lax.fori_loop(0, 8, four, 0)
        leave(i).start()
        return carry

    lax.fori_loop(0, pieces, pack, 0)

    def wait(i, carry):
        leave(i).wait()
        return carry

    lax.fori_loop(0, pieces, wait, 0)


def give(
    planes,
    od,
    acc,
    od_out,
    kvg,
    own,
    part,
    inbox,
    outbox,
    fin,
    spread,
    q_send,
    q_recv,
    pair_send,
    pair_recv,
    own_sem,
    ring_send,
    ring_recv,
    near_send,
    near_recv,
    mine_sem,
):
    x, y, z, core = place()
    half_way = planes // 2
    f32 = jnp.float32
    greet(planes, x, y, z, core)

    def chunk(d, s):
        far = half_way - s
        return (z + far) % planes if d == 0 else (z + planes - far) % planes

    def pair(at):
        return remote(
            acc.at[pl.ds(at * 16 + (1 - core) * 8, 8)],
            part.at[at],
            pair_send.at[at],
            pair_recv.at[at],
            ctx_of(z, y, 1 - core),
            x,
        )

    def load(at):
        return pltpu.make_async_copy(
            acc.at[pl.ds(at * 16 + core * 8, 8)], own.at[at], own_sem.at[at]
        )

    def hop(d, s, half):
        to = (z + 1) % planes if d == 0 else (z + planes - 1) % planes
        return remote(
            outbox.at[d, s, half],
            inbox.at[d, s, half],
            ring_send.at[d, s, half],
            ring_recv.at[d, s, half],
            ctx_of(to, y, core),
            x,
        )

    def answer(k):
        t = (x * SIDE + y + k) % PLANE
        return remote(
            od.at[t],
            od_out.at[unit_of(x, y)],
            q_send.at[k - 1],
            q_recv.at[k - 1],
            ctx_of(z, t % SIDE, core),
            t // SIDE,
        )

    def near(d):
        to = (y + d) % SIDE
        return remote(
            fin.at[pl.ds(to * 2, 2)],
            spread.at[y],
            near_send.at[d - 1],
            near_recv.at[d - 1],
            ctx_of(z, to, core),
            x,
        )

    def begin(at):
        pair(at).start()
        load(at).start()

    def ready(at):
        load(at).wait()
        pair(at).wait_recv()

    def here(at, half):
        span = pl.ds(half * 4, 4)
        return own[at, span].astype(f32) + part[at, span].astype(f32)

    def emit(d, s, half, extra):
        total = here(chunk(d, s), half)
        if extra:
            hop(d, s - 1, half).wait_recv()
            total += inbox[d, s - 1, half].astype(f32)
        outbox[d, s, half] = total.astype(jnp.bfloat16)
        hop(d, s, half).start()

    begin(chunk(0, 0))

    def begin_step(s, carry):
        begin(chunk(0, s))
        begin(chunk(1, s))
        return carry

    lax.fori_loop(1, half_way, begin_step, 0)
    begin(z)

    home = pltpu.make_async_copy(od.at[x * SIDE + y], od_out.at[unit_of(x, y)], mine_sem)
    home.start()

    def send_answer(k, carry):
        answer(k).start()
        return carry

    lax.fori_loop(1, PLANE, send_answer, 0)

    ready(chunk(0, 0))
    for d in range(2):
        emit(d, 0, d, False)
    for d in range(2):
        ready(chunk(d, 1))
        for half in range(2):
            emit(d, 1, half, half == d)

    def step(s, carry):
        for d in range(2):
            ready(chunk(d, s))
        for half in range(2):
            for d in range(2):
                emit(d, s, half, True)
        return carry

    lax.fori_loop(2, half_way, step, 0)
    ready(z)
    for half in range(2):
        total = here(z, half)
        for d in range(2):
            hop(d, half_way - 1, half).wait_recv()
            total += inbox[d, half_way - 1, half].astype(f32)
        fin[pl.ds(half * 4, 4)] = total.astype(jnp.bfloat16)
    for d in range(1, SIDE):
        near(d).start()
    spread[y] = fin[pl.ds(y * 2, 2)]

    def finish(s, carry):
        for d in range(2):
            for half in range(2):
                hop(d, s, half).wait_send()
        return carry

    lax.fori_loop(1, half_way, finish, 0)
    for d in range(2):
        hop(d, 0, d).wait_send()

    def finish_pair(at, carry):
        pair(at).wait_send()
        return carry

    lax.fori_loop(0, planes, finish_pair, 0)

    def finish_answer(k, carry):
        answer(k).wait()
        return carry

    lax.fori_loop(1, PLANE, finish_answer, 0)
    home.wait()
    for d in range(1, SIDE):
        near(d).wait()
    for pick in range(2):
        kvg[pick] = (spread[2 * pick].astype(f32) + spread[2 * pick + 1].astype(f32)).astype(
            jnp.bfloat16
        )


def local(planes, queries, key_states, value_states, grad_out, selected):
    bf16 = jnp.bfloat16
    dma = pltpu.SemaphoreType.DMA
    half_way = planes // 2
    x = lax.axis_index("head")
    ctx = lax.axis_index("ctx")
    heads = queries.shape[1]

    qd = (
        jnp.stack([queries, grad_out])
        .reshape(2, 2, BLOCK, heads, HEAD)
        .transpose(1, 3, 0, 2, 4)
        .reshape(PLANE, 2, BLOCK, HEAD)
    )
    kv = (
        lax.dynamic_slice_in_dim(jnp.stack([key_states, value_states]), 2 * x, 2, 2)
        .reshape(2, 2, BLOCK, 2, HEAD)
        .transpose(3, 1, 0, 2, 4)
    )
    sel = lax.dynamic_slice_in_dim(selected, 2 * ctx, 2, 0).reshape(PLANE, 1, 3)
    sel = jnp.pad(sel, ((0, 0), (0, 0), (0, HEAD - 3)))

    shape = jax.ShapeDtypeStruct
    units = shape((PLANE, 2, BLOCK, HEAD), bf16)
    rows = shape((planes * 16, 2, BLOCK, HEAD), bf16)

    qd_all, sel_all, store = pl.pallas_call(
        functools.partial(bring, planes),
        name="bring",
        out_shape=(units, shape((PLANE, 1, HEAD), jnp.int32), rows),
        in_specs=[VMEM, VMEM, VMEM],
        out_specs=(ANY, ANY, ANY),
        scratch_shapes=[
            dma((SIDE - 1,)),
            dma((SIDE - 1,)),
            dma((PLANE - 1,)),
            dma((PLANE - 1,)),
            dma((PLANE - 1,)),
            dma((PLANE - 1,)),
            dma((2, half_way, 2)),
            dma((2, half_way, 2)),
            dma((2, half_way + 1, 2)),
            dma((2, half_way + 1, 2)),
            dma((3,)),
        ],
        compiler_params=pltpu.CompilerParams(collective_id=0, has_side_effects=True),
    )(qd, sel, kv)

    od, acc = pl.pallas_call(
        attend,
        name="attend",
        out_shape=(units, rows),
        in_specs=[SMEM, VMEM, ANY],
        out_specs=(VMEM, ANY),
        scratch_shapes=[
            pltpu.VMEM((PLANE, 4, 2, BLOCK, HEAD), bf16),
            pltpu.VMEM((planes * 16, 2, BLOCK, HEAD), jnp.float32),
            pltpu.VMEM((planes * 16, 2, BLOCK, HEAD), bf16),
            dma((PLANE,)),
            dma((planes,)),
        ],
        compiler_params=pltpu.CompilerParams(vmem_limit_bytes=48 * 1024 * 1024),
    )(sel_all, qd_all, store)

    piece = (4, 2, BLOCK, HEAD)
    od_all, kvg = pl.pallas_call(
        functools.partial(give, planes),
        name="give",
        out_shape=(units, shape((2, 2, 2, BLOCK, HEAD), bf16)),
        in_specs=[VMEM, ANY],
        out_specs=(ANY, VMEM),
        scratch_shapes=[
            pltpu.VMEM((planes, 8, 2, BLOCK, HEAD), bf16),
            pltpu.VMEM((planes, 8, 2, BLOCK, HEAD), bf16),
            pltpu.VMEM((2, half_way, 2, *piece), bf16),
            pltpu.VMEM((2, half_way, 2, *piece), bf16),
            pltpu.VMEM((8, 2, BLOCK, HEAD), bf16),
            pltpu.VMEM((SIDE, 2, 2, BLOCK, HEAD), bf16),
            dma((PLANE - 1,)),
            dma((PLANE - 1,)),
            dma((planes,)),
            dma((planes,)),
            dma((planes,)),
            dma((2, half_way, 2)),
            dma((2, half_way, 2)),
            dma((SIDE - 1,)),
            dma((SIDE - 1,)),
            dma,
        ],
        compiler_params=pltpu.CompilerParams(
            collective_id=1, has_side_effects=True, vmem_limit_bytes=32 * 1024 * 1024
        ),
    )(od, acc)

    od_all = (
        od_all.reshape(2, heads, 2, BLOCK, HEAD)
        .transpose(2, 0, 3, 1, 4)
        .reshape(2, 2 * BLOCK, heads, HEAD)
    )
    kvg = kvg.transpose(2, 1, 3, 0, 4).reshape(2, 2 * BLOCK, 2, HEAD)
    return od_all[0], od_all[1], kvg[0], kvg[1]


def solution(mesh):
    planes = mesh.shape["ctx"] // (2 * SIDE)
    spread = P("ctx", "head", None)
    whole = P("ctx", None, None)
    return jax.shard_map(
        functools.partial(local, planes),
        mesh=mesh,
        in_specs=(spread, whole, whole, spread, P(None, "head", None)),
        out_specs=(spread, spread, spread, spread),
        check_vma=False,
    )
```

time: 480 us -> 166 us (0.35); the launches traced: 475 us -> 166 us
  waiting for transfers between devices: 363 us -> 0 us
  Pallas kernels: 0 us -> 151 us
  starting transfers between devices: 45 us -> 0 us
  local copies, waits for them, and re-layouts: 46.2 us -> 13.6 us
  matrix products: 10.2 us -> 0 us
  other arithmetic: 10.1 us -> 0.92 us
    all_to_all x4 -> x0, waiting for transfers between devices: 363 us -> none  [the longest x1 184 us: in_one_piece(): lax.all_to_all(both, axis, split_axis=split_dim, concat_axis=concat_dim,...]
    pallas_call x0 -> x3, Pallas kernels: none -> 151 us  [the longest x1 73 us: local(): pl.pallas_call(functools.partial(bring, planes), name='bring', out_shape=...]
    all_to_all x4 -> x0, starting transfers between devices: 45 us -> none  [the longest x1 20.6 us: in_one_piece(): lax.all_to_all(both, axis, split_axis=split_dim, concat_axis=concat_dim,...]
    scatter x2 -> x0, local copies, waits for them, and re-layouts: 13.2 us -> none  [local(): empty_slots.at[position]]
    dot_general x14 -> x0, matrix products: 10.2 us -> none  [the longest x1 2.29 us: local(): jnp.dot(collect_matrix, recv_key_terms.reshape(slot_count, BLOCK * head_s...]
    gather x4 -> x0, local copies, waits for them, and re-layouts: 7.83 us -> none  [the longest x1 3.14 us: local(): jnp.take(recv_values, position, axis=0)]
    reshape x7 -> x2, local copies, waits for them, and re-layouts: 8.61 us -> 0.8 us  [the longest x1 0.66 us: local(): kv = lax.dynamic_slice_in_dim(jnp.stack([key_states, value_states]), 2 *...]
  transfers between devices with their start and end apart: 4 -> 0, of which waited for: 4 -> 0; matrix products, arithmetic and copies ran while one was open for 5% -> 0% of each run, Pallas kernels for 0% -> 0%
where the time goes in v1:
time: 166 us
  Pallas kernels  151 us (91%)
  local copies, waits for them, and re-layouts  13.6 us (8%)
    pallas_call x1, Pallas kernels, local(): pl.pallas_call(functools.partial(bring, planes), name='bring', out_shape=...  73 us
    pallas_call x1, Pallas kernels, local(): pl.pallas_call(functools.partial(give, planes), name='give', out_shape=(u...  59.3 us
    pallas_call x1, Pallas kernels, local(): pl.pallas_call(attend, name='attend', out_shape=(units, rows), in_specs=[...  18.3 us
    unnamed x10, local copies, waits for them, and re-layouts  7.23 us

profile of v1, /device:TPU:6, one launch (start us, length us, event | category | flops | bytes accessed | tf_op | source)
XLA Modules:
  0.0 165.9 jit_solution(1943352300817098720)
XLA Ops:
  0.6 0.0 copy-start
  0.7 0.7 copy-done
  1.4 0.1 constant_dynamic-slice_fusion
  1.4 0.1 copy.28
  1.6 0.6 pad.4.sel
  2.2 1.0 copy.17
  3.2 1.0 copy.18
  4.2 0.9 pad_maximum_fusion
  5.1 1.1 copy_bitcast_fusion
  6.2 0.7 copy.33
  6.9 73.0 %bring.1 = (bf16[16,2,64,128]{3,2,1,0:T(8,128)(2,1)}, s32[16,1,128]{2,1,0:T(1,128)}, bf16[256,2,64,128]{3,2,1,0:T(8,128)(2,1)}) custom-call(bf16[16,2,64,128]{3,2,1,0:T(8,128)(2,1)} %bitcast.24, s32[16,1,128]{2,1,0:T(1,128)} %pad.4.sel, bf16[2,2,2,64,128]{4,3,2,1,0:T(8,128)(2,1)} %bitcast.25), custom_call_target="tpu_custom_call" | custom-call | tf_op jit(solution)/shard_map/bring/pallas_call | solution.py:533
  79.9 0.0 copy-start.2
  79.9 1.0 copy-done.2
  81.0 0.0 copy-start.3
  81.0 0.7 copy-done.3
  81.7 18.3 %attend.1 = (bf16[16,2,64,128]{3,2,1,0:T(8,128)(2,1)S(1)}, bf16[256,2,64,128]{3,2,1,0:T(8,128)(2,1)}) custom-call(s32[16,1,128]{2,1,0:T(1,128)S(1)} %copy-done.3, bf16[16,2,64,128]{3,2,1,0:T(8,128)(2,1)S(1)} %copy-done.2, bf16[256,2,64,128]{3,2,1,0:T(8,128)(2,1)} %get-tuple-element.13.store), custom_call_target="tpu_custom_call" | custom-call | tf_op jit(solution)/shard_map/attend/pallas_call | solution.py:555
  100.0 0.0 copy-start.1
  100.0 3.4 %copy-done.1 = bf16[256,2,64,128]{3,2,1,0:T(8,128)(2,1)S(1)} copy-done((bf16[256,2,64,128]{3,2,1,0:T(8,128)(2,1)S(1)}, bf16[256,2,64,128]{3,2,1,0:T(8,128)(2,1)}, u32[]{:S(2)}) %copy-start.1) | copy-done | bytes 8388632
  103.4 59.3 %give.1 = (bf16[16,2,64,128]{3,2,1,0:T(8,128)(2,1)S(1)}, bf16[2,2,2,64,128]{4,3,2,1,0:T(8,128)(2,1)S(1)}) custom-call(bf16[16,2,64,128]{3,2,1,0:T(8,128)(2,1)S(1)} %get-tuple-element.14.od, bf16[256,2,64,128]{3,2,1,0:T(8,128)(2,1)S(1)} %copy-done.1), custom_call_target="tpu_custom_call" | custom-call | tf_op jit(solution)/shard_map/give/pallas_call | solution.py:572
  162.7 0.7 copy.27
  163.4 0.7 copy.26
  164.2 0.9 copy.25
  165.0 0.9 copy.24
  (3 shorter events, 0.1 us)
Async XLA Ops:
  0.6 0.7 copy-start
  79.9 1.0 copy-start.2
  81.0 0.7 copy-start.3
  100.0 3.4 %copy-start.1 = (bf16[256,2,64,128]{3,2,1,0:T(8,128)(2,1)S(1)}, bf16[256,2,64,128]{3,2,1,0:T(8,128)(2,1)}, u32[]{:S(2)}) copy-start(bf16[256,2,64,128]{3,2,1,0:T(8,128)(2,1)} %get-tuple-element.15.acc) | copy-start | bytes 25165828

commit v2 on v1

v2 whole, which is shorter than its diff:
```python
import functools

import jax
import jax.numpy as jnp
from jax import lax
from jax.experimental import pallas as pl
from jax.experimental.pallas import tpu as pltpu
from jax.sharding import PartitionSpec as P

BLOCK = 64
HEAD = 128
SIDE = 4
PLANE = SIDE * SIDE
MESH = pl.DeviceIdType.MESH
VMEM = pl.BlockSpec(memory_space=pltpu.VMEM)
SMEM = pl.BlockSpec(memory_space=pltpu.SMEM)
HBM = pl.BlockSpec(memory_space=pltpu.HBM)

HALVES = ((0, 1), (2, 1))


def place():
    ctx = lax.axis_index("ctx")
    x = lax.axis_index("head")
    return x, (ctx // 2) % SIDE, ctx // (2 * SIDE), ctx % 2


def ctx_of(z, y, core):
    return (z * SIDE + y) * 2 + core


def unit_of(x, y):
    return (y % 2) * 8 + 2 * x + y // 2


def piece_of(parity, i):
    return (3 * parity, parity + 1, 2 - parity)[i]


def greet(planes, x, y, z, core):
    barrier = pltpu.get_barrier_semaphore()

    def one(k, carry):
        t = (x * SIDE + y + k) % PLANE
        pl.semaphore_signal(
            barrier, inc=1, device_id=(ctx_of(z, t % SIDE, core), t // SIDE), device_id_type=MESH
        )
        return carry

    for other in (
        ctx_of((z + 1) % planes, y, core),
        ctx_of((z + planes - 1) % planes, y, core),
        ctx_of(z, y, 1 - core),
        ctx_of(z, y + 1 - 2 * (y % 2), 1 - core),
    ):
        pl.semaphore_signal(barrier, inc=1, device_id=(other, x), device_id_type=MESH)
    lax.fori_loop(1, PLANE, one, 0)
    pl.semaphore_wait(barrier, PLANE + 3)


def remote(src, dst, send, recv, ctx, x):
    return pltpu.make_async_remote_copy(
        src_ref=src, dst_ref=dst, send_sem=send, recv_sem=recv, device_id=(ctx, x), device_id_type=MESH
    )


def bring(
    planes,
    q_hbm,
    g_hbm,
    k_hbm,
    v_hbm,
    sel_hbm,
    qd_out,
    sel_out,
    store,
    q,
    g,
    k,
    v,
    sel,
    qd,
    kv,
    sel_all,
    load_sem,
    near_send,
    near_recv,
    q_send,
    q_recv,
    i_send,
    i_recv,
    ring_send,
    ring_recv,
    pair_send,
    pair_recv,
    mate_send,
    mate_recv,
    over_send,
    over_recv,
    own_sem,
):
    x, y, z, core = place()
    half_way = planes // 2
    last = half_way - 1
    parity = y % 2
    mate = y + 1 - 2 * parity
    heads = q.shape[1]

    loads = [
        pltpu.make_async_copy(src, dst, load_sem.at[i])
        for i, (src, dst) in enumerate(
            ((k_hbm, k), (v_hbm, v), (q_hbm, q), (g_hbm, g), (sel_hbm, sel))
        )
    ]
    for copy in loads:
        copy.start()
    for copy in loads[:2]:
        copy.wait()
    for b in range(2):
        tokens = pl.ds(b * BLOCK, BLOCK)
        kv[:, b, 0] = jnp.swapaxes(k[tokens], 0, 1)
        kv[:, b, 1] = jnp.swapaxes(v[tokens], 0, 1)
    greet(planes, x, y, z, core)

    def near(d):
        to = (y + d) % SIDE
        return remote(
            kv.at[2 * x + to // 2],
            store.at[pl.ds(z * 16 + core * 8 + y * 2, 2)],
            near_send.at[d - 1],
            near_recv.at[d - 1],
            ctx_of(z, to, core),
            x,
        )

    def query(i):
        t = (x * SIDE + y + i) % PLANE
        return remote(
            qd.at[unit_of(t // SIDE, t % SIDE)],
            qd_out.at[x * SIDE + y],
            q_send.at[i - 1],
            q_recv.at[i - 1],
            ctx_of(z, t % SIDE, core),
            t // SIDE,
        )

    def index(d):
        return remote(
            sel, sel_all.at[x], i_send.at[d - 1], i_recv.at[d - 1], ctx_of(z, y, core), (x + d) % SIDE
        )

    def at(d, j, side, first, count):
        origin = (z + planes - j) % planes if d == 0 else (z + j) % planes
        return store.at[pl.ds(origin * 16 + side * 8 + first, count)]

    def piece(d, j, side, i, split):
        first = 2 * piece_of(parity, i)
        if split and i == 1:
            return at(d, j, side, first + d, 1)
        return at(d, j, side, first, 2)

    def hop(d, s, i, split=False):
        to = (z + 1) % planes if d == 0 else (z + planes - 1) % planes
        part = piece(d, s - 1, core, i, split)
        sems = ring_send.at[d, s - 1, i], ring_recv.at[d, s - 1, i]
        return remote(part, part, *sems, ctx_of(to, y, core), x)

    def arrived(d, s, i, split=False):
        part = piece(d, s, core, i, split)
        sems = ring_send.at[d, s - 1, i], ring_recv.at[d, s - 1, i]
        return remote(part, part, *sems, ctx_of(z, y, 1 - core), x)

    def share(d, s, i, side, split=False):
        part = piece(d, s, side, i, split)
        sems = pair_send.at[d, s - 1, i], pair_recv.at[d, s - 1, i]
        return remote(part, part, *sems, ctx_of(z, y, 1 - core), x)

    def share_own(side):
        part = at(0, 0, side, 0, 8)
        sems = own_sem.at[1], own_sem.at[2]
        return remote(part, part, *sems, ctx_of(z, y, 1 - core), x)

    def cross(d, s, first):
        part = at(d, s, core, 6 * first, 2)
        sems = mate_send.at[d, s - 1], mate_recv.at[d, s - 1]
        return remote(part, part, *sems, ctx_of(z, mate, core), x)

    def over(d, s, side):
        part = at(d, s, side, 6 * (1 - parity), 2)
        sems = over_send.at[d, s - 1], over_recv.at[d, s - 1]
        return remote(part, part, *sems, ctx_of(z, y, 1 - core), x)

    def cross_over(first, side):
        part = at(0, half_way, side, 6 * first, 2)
        sems = over_send.at[0, last], over_recv.at[0, last]
        return remote(part, part, *sems, ctx_of(z, mate, 1 - core), x)

    for d in range(1, SIDE):
        near(d).start()
    mine = pltpu.make_async_copy(
        kv.at[2 * x + y // 2], store.at[pl.ds(z * 16 + core * 8 + y * 2, 2)], own_sem.at[0]
    )
    mine.start()
    for copy in loads[2:]:
        copy.wait()
    for d in range(1, SIDE):
        index(d).start()
    for b in range(2):
        tokens = pl.ds(b * BLOCK, BLOCK)
        units = pl.ds(b * heads, heads)
        qd[units, 0] = jnp.swapaxes(q[tokens], 0, 1)
        qd[units, 1] = jnp.swapaxes(g[tokens], 0, 1)
    mine.wait()
    for d in range(1, SIDE):
        near(d).wait_recv()
    for i in range(3):
        for d in range(2):
            hop(d, 1, i).start()
    share_own(core).start()

    def send_query(i, carry):
        query(i).start()
        return carry

    lax.fori_loop(1, PLANE, send_query, 0)
    qd_out[x * SIDE + y] = qd[unit_of(x, y)]
    sel_all[x] = sel[...]

    def step(s, carry):
        for i in range(3):
            for d in range(2):
                arrived(d, s - 1, i).wait_recv()
                hop(d, s, i).start()
                if i == 0:
                    cross(d, s - 1, parity).start()
                share(d, s - 1, i, core).start()

        @pl.when(s > 2)
        def _():
            for d in range(2):
                cross(d, s - 2, 1 - parity).wait_recv()
                over(d, s - 2, core).start()

        return carry

    lax.fori_loop(2, half_way, step, 0)
    for i in range(3):
        for d in range(2):
            arrived(d, last, i).wait_recv()
            if i in HALVES[d]:
                hop(d, half_way, i, True).start()
            if i == 0:
                cross(d, last, parity).start()
            share(d, last, i, core).start()
    for d in range(2):
        cross(d, last - 1, 1 - parity).wait_recv()
        over(d, last - 1, core).start()
    for k in range(2):
        for d in range(2):
            i = HALVES[d][k]
            arrived(d, half_way, i, True).wait_recv()
            if i == 0:
                cross(0, half_way, parity).start()
                cross_over(parity, core).start()
            share(d, half_way, i, core, True).start()
    for d in range(2):
        cross(d, last, 1 - parity).wait_recv()
        over(d, last, core).start()

    def finish_query(i, carry):
        query(i).wait()
        return carry

    lax.fori_loop(1, PLANE, finish_query, 0)
    for d in range(1, SIDE):
        index(d).wait()
    own_head = lax.broadcasted_iota(jnp.int32, sel.shape, 1) == 2 * x + y // 2
    for group in range(SIDE):
        sel_out[group] = jnp.sum(jnp.where(own_head, sel_all[group], 0), axis=1)

    for d in range(1, SIDE):
        near(d).wait_send()
    share_own(1 - core).wait_recv()
    share_own(core).wait_send()

    def finish(s, carry):
        for d in range(2):
            for i in range(3):
                hop(d, s, i).wait_send()
                share(d, s, i, 1 - core).wait_recv()
                share(d, s, i, core).wait_send()
            cross(d, s, parity).wait_send()
            over(d, s, 1 - core).wait_recv()
            over(d, s, core).wait_send()
        return carry

    lax.fori_loop(1, half_way, finish, 0)
    for d in range(2):
        for i in HALVES[d]:
            hop(d, half_way, i, True).wait_send()
            share(d, half_way, i, 1 - core, True).wait_recv()
            share(d, half_way, i, core, True).wait_send()
    cross(0, half_way, parity).wait_send()
    cross_over(parity, core).wait_send()
    cross(0, half_way, 1 - parity).wait_recv()
    cross_over(1 - parity, 1 - core).wait_recv()


def attend(sel, qd, store, od, acc):
    x, y, z, core = place()
    parity = y % 2
    factor = HEAD**-0.5
    f32, bf16 = jnp.float32, jnp.bfloat16
    nt = (((1,), (1,)), ((), ()))
    nn = (((1,), (0,)), ((), ()))
    tn = (((0,), (0,)), ((), ()))

    def clear(i, carry):
        acc[pl.ds(i * 4, 4)] = jnp.zeros((4, 2, BLOCK, HEAD), bf16)
        return carry

    lax.fori_loop(0, acc.shape[0] // 4, clear, 0)

    def dot(a, b, dims):
        return lax.dot_general(a, b, dims, preferred_element_type=f32)

    def one(side, carry):
        own = z * 16 + core * 8 + side * 2 + parity
        block = ((z * SIDE + side) * 2 + core) * 2 + parity
        own_terms = [jnp.zeros((BLOCK, HEAD), f32)] * 2
        for group in range(SIDE):
            u = group * SIDE + side
            rows = [own]
            for t in range(3):
                n = sel[group, t, block]
                rows.append((n // 16) * 16 + ((n // 2) % 2) * 8 + ((n // 4) % SIDE) * 2 + n % 2)
            q = qd[u, 0]
            g = qd[u, 1]
            keys = jnp.concatenate([store[r, 0] for r in rows], axis=0)
            values = jnp.concatenate([store[r, 1] for r in rows], axis=0)
            scores = dot(q, keys, nt) * factor
            top = jnp.max(scores, axis=1, keepdims=True)
            e = jnp.exp(scores - top)
            prob = e * (1.0 / jnp.sum(e, axis=1, keepdims=True))
            prob_b = prob.astype(bf16)
            out = dot(prob_b, values, nn).astype(bf16)
            od[u, 0] = out
            delta = jnp.sum(g.astype(f32) * out.astype(f32), axis=1, keepdims=True)
            grad_prob = dot(g, values, nt)
            grad_scores = (prob * (grad_prob - delta)).astype(bf16)
            od[u, 1] = (dot(grad_scores, keys, nn) * factor).astype(bf16)
            terms = dot(grad_scores, q, tn) * factor, dot(prob_b, g, tn)
            for i in range(2):
                own_terms[i] += terms[i][:BLOCK]
                for t in range(1, 4):
                    part = terms[i][t * BLOCK : (t + 1) * BLOCK]
                    acc[rows[t], i] = (acc[rows[t], i].astype(f32) + part).astype(bf16)
        for i in range(2):
            acc[own, i] = (acc[own, i].astype(f32) + own_terms[i]).astype(bf16)
        return carry

    lax.fori_loop(0, SIDE, one, 0)


def give(
    planes,
    od,
    acc,
    att,
    grad_q,
    kvg,
    part,
    inbox,
    outbox,
    mate_in,
    mate_out,
    fin,
    spread,
    od_all,
    q_send,
    q_recv,
    pair_send,
    pair_recv,
    mate_send,
    mate_recv,
    ring_send,
    ring_recv,
    near_send,
    near_recv,
    mine_sem,
):
    x, y, z, core = place()
    half_way = planes // 2
    parity = y % 2
    mate = y + 1 - 2 * parity
    heads = att.shape[1]
    f32, bf16 = jnp.float32, jnp.bfloat16

    for d in range(2):
        inbox[d, 0, 1, 1 - d] = jnp.zeros((2, BLOCK, HEAD), bf16)
    greet(planes, x, y, z, core)

    def chunk(d, s):
        far = half_way - s
        return (z + far) % planes if d == 0 else (z + planes - far) % planes

    def pair(at):
        return remote(
            acc.at[pl.ds(at * 16 + (1 - core) * 8, 8)],
            part.at[at],
            pair_send.at[at],
            pair_recv.at[at],
            ctx_of(z, y, 1 - core),
            x,
        )

    def cross(at):
        return remote(
            mate_out.at[at],
            mate_in.at[at],
            mate_send.at[at],
            mate_recv.at[at],
            ctx_of(z, mate, core),
            x,
        )

    def hop(d, s, i):
        to = (z + 1) % planes if d == 0 else (z + planes - 1) % planes
        box = (d, s, i, pl.ds(d, 1)) if isinstance(s, int) and s == 0 and i == 1 else (d, s, i)
        return remote(
            outbox.at[box],
            inbox.at[box],
            ring_send.at[d, s, i],
            ring_recv.at[d, s, i],
            ctx_of(to, y, core),
            x,
        )

    def answer(i):
        t = (x * SIDE + y + i) % PLANE
        return remote(
            od.at[t],
            od_all.at[unit_of(x, y)],
            q_send.at[i - 1],
            q_recv.at[i - 1],
            ctx_of(z, t % SIDE, core),
            t // SIDE,
        )

    def near(d):
        to = (y + d) % SIDE
        return remote(
            fin.at[pl.ds(to * 2, 2)],
            spread.at[y],
            near_send.at[d - 1],
            near_recv.at[d - 1],
            ctx_of(z, to, core),
            x,
        )

    def chip_sum(at, first, count):
        mine = acc[pl.ds(at * 16 + core * 8 + first, count)].astype(f32)
        return mine + part[at, pl.ds(first, count)].astype(f32)

    def prepare(at):
        pair(at).wait_recv()
        mate_out[at] = chip_sum(at, 6 * (1 - parity), 2).astype(bf16)
        cross(at).start()

    def emit(d, s, i, extra):
        at = chunk(d, s)
        total = chip_sum(at, 2 * piece_of(parity, i), 2)
        if i == 0:
            total += mate_in[at].astype(f32)
        if extra:
            hop(d, s - 1, i).wait_recv()
            total += inbox[d, s - 1, i].astype(f32)
        outbox[d, s, i] = total.astype(bf16)
        hop(d, s, i).start()

    pair(chunk(0, 0)).start()

    def begin_step(s, carry):
        pair(chunk(0, s)).start()
        pair(chunk(1, s)).start()
        return carry

    lax.fori_loop(1, half_way, begin_step, 0)
    pair(z).start()

    home = pltpu.make_async_copy(od.at[x * SIDE + y], od_all.at[unit_of(x, y)], mine_sem)
    home.start()

    def send_answer(i, carry):
        answer(i).start()
        return carry

    prepare(chunk(0, 0))
    for d in range(2):
        emit(d, 0, 1, False)
    emit(1, 0, 2, False)
    for d in range(2):
        prepare(chunk(d, 1))
    cross(chunk(0, 0)).wait_recv()
    emit(0, 0, 0, False)
    lax.fori_loop(1, PLANE, send_answer, 0)
    for d in range(2):
        prepare(chunk(d, 2))
    for i in (2, 1, 0):
        for d in range(2):
            if i == 0:
                cross(chunk(d, 1)).wait_recv()
            emit(d, 1, i, i in HALVES[d])

    def step(s, carry):
        @pl.when(s + 1 < half_way)
        def _():
            for d in range(2):
                prepare(chunk(d, s + 1))

        for i in (2, 1, 0):
            for d in range(2):
                if i == 0:
                    cross(chunk(d, s)).wait_recv()
                emit(d, s, i, True)
        return carry

    lax.fori_loop(2, half_way, step, 0)

    def finish_answer(i, carry):
        answer(i).wait()
        return carry

    lax.fori_loop(1, PLANE, finish_answer, 0)
    home.wait()
    for b in range(2):
        tokens = pl.ds(b * BLOCK, BLOCK)
        units = pl.ds(b * heads, heads)
        att[tokens] = jnp.swapaxes(od_all[units, 0], 0, 1)
        grad_q[tokens] = jnp.swapaxes(od_all[units, 1], 0, 1)

    pair(z).wait_recv()
    rest = 6 * (1 - parity)
    fin[pl.ds(rest, 2)] = chip_sum(z, rest, 2).astype(bf16)
    for i in (2, 1, 0):
        first = 2 * piece_of(parity, i)
        total = chip_sum(z, first, 2)
        for d in range(2):
            hop(d, half_way - 1, i).wait_recv()
            total += inbox[d, half_way - 1, i].astype(f32)
        fin[pl.ds(first, 2)] = total.astype(bf16)
    for d in range(1, SIDE):
        near(d).start()
    spread[y] = fin[pl.ds(y * 2, 2)]

    def finish(s, carry):
        for d in range(2):
            for i in range(3):
                hop(d, s, i).wait_send()
            cross(chunk(d, s)).wait_send()
            pair(chunk(d, s)).wait_send()
        return carry

    lax.fori_loop(1, half_way, finish, 0)
    for d in range(2):
        for i in HALVES[d]:
            hop(d, 0, i).wait_send()
    cross(chunk(0, 0)).wait_send()
    pair(chunk(0, 0)).wait_send()
    pair(z).wait_send()

    for d in range(1, SIDE):
        near(d).wait()
    for pick in range(2):
        kvg[pick] = (spread[2 * pick].astype(f32) + spread[2 * pick + 1].astype(f32)).astype(bf16)


def leave(att, grad_q, kvg, att_out, grad_q_out, grad_k_out, grad_v_out, pair, sem):
    copies = [
        pltpu.make_async_copy(src, dst, sem.at[i])
        for i, (src, dst) in enumerate(
            (
                (att, att_out),
                (grad_q, grad_q_out),
                (pair.at[0], grad_k_out),
                (pair.at[1], grad_v_out),
            )
        )
    ]
    for copy in copies[:2]:
        copy.start()
    for b in range(2):
        for i in range(2):
            pair[i, pl.ds(b * BLOCK, BLOCK)] = jnp.swapaxes(kvg[:, b, i], 0, 1)
    for copy in copies[2:]:
        copy.start()
    for copy in copies:
        copy.wait()


def local(planes, queries, key_states, value_states, grad_out, selected):
    bf16 = jnp.bfloat16
    dma = pltpu.SemaphoreType.DMA
    half_way = planes // 2
    heads = queries.shape[1]
    blocks = selected.shape[0]

    shape = jax.ShapeDtypeStruct
    units = (PLANE, 2, BLOCK, HEAD)
    rows = (planes * 16, 2, BLOCK, HEAD)
    lists = (3, heads, blocks)
    given = queries, grad_out, key_states, value_states, selected.transpose(2, 1, 0)

    qd, sel, store = pl.pallas_call(
        functools.partial(bring, planes),
        name="bring",
        out_shape=(shape(units, bf16), shape((SIDE, 3, blocks), jnp.int32), shape(rows, bf16)),
        in_specs=[HBM] * 5,
        out_specs=(VMEM,) * 3,
        scratch_shapes=[
            pltpu.VMEM(queries.shape, bf16),
            pltpu.VMEM(queries.shape, bf16),
            pltpu.VMEM(queries.shape, bf16),
            pltpu.VMEM(queries.shape, bf16),
            pltpu.VMEM(lists, jnp.int32),
            pltpu.VMEM(units, bf16),
            pltpu.VMEM((heads, 2, 2, BLOCK, HEAD), bf16),
            pltpu.VMEM((SIDE, *lists), jnp.int32),
            dma((5,)),
            dma((SIDE - 1,)),
            dma((SIDE - 1,)),
            dma((PLANE - 1,)),
            dma((PLANE - 1,)),
            dma((SIDE - 1,)),
            dma((SIDE - 1,)),
            dma((2, half_way, 3)),
            dma((2, half_way, 3)),
            dma((2, half_way, 3)),
            dma((2, half_way, 3)),
            dma((2, half_way)),
            dma((2, half_way)),
            dma((2, half_way)),
            dma((2, half_way)),
            dma((3,)),
        ],
        compiler_params=pltpu.CompilerParams(
            collective_id=0, has_side_effects=True, vmem_limit_bytes=16 * 1024 * 1024
        ),
    )(*(pltpu.with_memory_space_constraint(a, pltpu.HBM) for a in given))

    od, acc = pl.pallas_call(
        attend,
        name="attend",
        out_shape=(shape(units, bf16), shape(rows, bf16)),
        in_specs=[SMEM, VMEM, VMEM],
        out_specs=(VMEM, VMEM),
        compiler_params=pltpu.CompilerParams(vmem_limit_bytes=24 * 1024 * 1024),
    )(sel, qd, store)

    piece = (3, 2, 2, BLOCK, HEAD)
    att, grad_q, kvg = pl.pallas_call(
        functools.partial(give, planes),
        name="give",
        out_shape=(
            shape(queries.shape, bf16),
            shape(queries.shape, bf16),
            shape((2, 2, 2, BLOCK, HEAD), bf16),
        ),
        in_specs=[VMEM, VMEM],
        out_specs=(VMEM,) * 3,
        scratch_shapes=[
            pltpu.VMEM((planes, 8, 2, BLOCK, HEAD), bf16),
            pltpu.VMEM((2, half_way, *piece), bf16),
            pltpu.VMEM((2, half_way, *piece), bf16),
            pltpu.VMEM((planes, 2, 2, BLOCK, HEAD), bf16),
            pltpu.VMEM((planes, 2, 2, BLOCK, HEAD), bf16),
            pltpu.VMEM((8, 2, BLOCK, HEAD), bf16),
            pltpu.VMEM((SIDE, 2, 2, BLOCK, HEAD), bf16),
            pltpu.VMEM(units, bf16),
            dma((PLANE - 1,)),
            dma((PLANE - 1,)),
            dma((planes,)),
            dma((planes,)),
            dma((planes,)),
            dma((planes,)),
            dma((2, half_way, 3)),
            dma((2, half_way, 3)),
            dma((SIDE - 1,)),
            dma((SIDE - 1,)),
            dma,
        ],
        compiler_params=pltpu.CompilerParams(
            collective_id=1, has_side_effects=True, vmem_limit_bytes=28 * 1024 * 1024
        ),
    )(od, acc)

    key_shape = (2 * BLOCK, 2, HEAD)
    return pl.pallas_call(
        leave,
        name="leave",
        out_shape=(
            shape(queries.shape, bf16),
            shape(queries.shape, bf16),
            shape(key_shape, bf16),
            shape(key_shape, bf16),
        ),
        in_specs=[VMEM] * 3,
        out_specs=(HBM,) * 4,
        scratch_shapes=[pltpu.VMEM((2, *key_shape), bf16), dma((4,))],
        compiler_params=pltpu.CompilerParams(vmem_limit_bytes=4 * 1024 * 1024),
    )(att, grad_q, kvg)


def solution(mesh):
    planes = mesh.shape["ctx"] // (2 * SIDE)
    spread = P("ctx", "head", None)
    whole = P("ctx", None, None)
    return jax.shard_map(
        functools.partial(local, planes),
        mesh=mesh,
        in_specs=(spread, whole, whole, spread, P(None, "head", None)),
        out_specs=(spread, spread, spread, spread),
        check_vma=False,
    )
```

time: 166 us -> 124 us (0.75)
  Pallas kernels: 151 us -> 123 us
  local copies, waits for them, and re-layouts: 13.6 us -> 0 us
    pallas_call x1, Pallas kernels: 73 us -> 57.1 us  [local(): pl.pallas_call(functools.partial(bring, planes), name='bring', out_shape=...]
    pallas_call x2 -> x3, Pallas kernels: 77.6 us -> 66 us  [the longest x1 52.5 us: local(): pl.pallas_call(functools.partial(give, planes), name='give', out_shape=(s...]
    unnamed x10 -> x0, local copies, waits for them, and re-layouts: 7.23 us -> none
    another operation x3 -> x0, local copies, waits for them, and re-layouts: 3.1 us -> none  [the longest x2 1.98 us: local(): jnp.stack([queries, grad_out]).reshape(2, 2, BLOCK, heads, HEAD)]
    slice x4 -> x0, local copies, waits for them, and re-layouts: 1.8 us -> none  [local(): return (od_all[0], od_all[1], kvg[0], kvg[1])]
where the time goes in v2:
time: 124 us
  Pallas kernels  123 us (99%)
    pallas_call x1, Pallas kernels, local(): pl.pallas_call(functools.partial(bring, planes), name='bring', out_shape=...  57.1 us
    pallas_call x1, Pallas kernels, local(): pl.pallas_call(functools.partial(give, planes), name='give', out_shape=(s...  52.5 us
    pallas_call x1, Pallas kernels, local(): pl.pallas_call(attend, name='attend', out_shape=(shape(units, bf16), shap...  12.6 us

profile of v2, /device:TPU:6, one launch (start us, length us, event | category | flops | bytes accessed | tf_op | source)
XLA Modules:
  0.0 123.8 jit_solution(7144763614283562035)
XLA Ops:
  0.6 57.1 %bring.1 = (bf16[16,2,64,128]{3,2,1,0:T(8,128)(2,1)S(1)}, s32[4,3,256]{2,1,0:T(4,128)S(1)}, bf16[256,2,64,128]{3,2,1,0:T(8,128)(2,1)S(1)}) custom-call(bf16[128,8,128]{2,1,0:T(8,128)(2,1)} %q_hbm.1, bf16[128,8,128]{2,1,0:T(8,128)(2,1)} %g_hbm.1, bf16[128,8,128]{2,1,0:T(8,128)(2,1)} %k_hbm.1, bf16[128,8,128]{2,1,0:T(8,128)(2,1)} %v_hbm.1, s32[3,8,256]{2,1,0:T(8,128)} %bitcast.1), custom_call_target="tpu_custom_call" | custom-call | tf_op jit(solution)/shard_map/bring/pallas_call | solution.py:614
  57.8 12.6 %attend.1 = (bf16[16,2,64,128]{3,2,1,0:T(8,128)(2,1)S(1)}, bf16[256,2,64,128]{3,2,1,0:T(8,128)(2,1)S(1)}) custom-call(s32[4,3,256]{2,1,0:T(4,128)S(1)} %get-tuple-element.12.sel, bf16[16,2,64,128]{3,2,1,0:T(8,128)(2,1)S(1)} %get-tuple-element.13.qd, bf16[256,2,64,128]{3,2,1,0:T(8,128)(2,1)S(1)} %get-tuple-element.14.store), custom_call_target="tpu_custom_call" | custom-call | tf_op jit(solution)/shard_map/attend/pallas_call | solution.py:651
  70.4 52.5 %give.1 = (bf16[128,8,128]{2,1,0:T(8,128)(2,1)S(1)}, bf16[128,8,128]{2,1,0:T(8,128)(2,1)S(1)}, bf16[2,2,2,64,128]{4,3,2,1,0:T(8,128)(2,1)S(1)}) custom-call(bf16[16,2,64,128]{3,2,1,0:T(8,128)(2,1)S(1)} %get-tuple-element.15.od, bf16[256,2,64,128]{3,2,1,0:T(8,128)(2,1)S(1)} %get-tuple-element.16.acc), custom_call_target="tpu_custom_call" | custom-call | tf_op jit(solution)/shard_map/give/pallas_call | solution.py:661
  122.9 0.9 leave.1

commit v3 on v2

--- a/solution.py
+++ b/solution.py
@@ -1,4 +1,5 @@
 import functools
+import math
 
 import jax
 import jax.numpy as jnp
@@ -37,7 +38,7 @@
     return (3 * parity, parity + 1, 2 - parity)[i]
 
 
-def greet(planes, x, y, z, core):
+def announce(planes, x, y, z, core):
     barrier = pltpu.get_barrier_semaphore()
 
     def one(k, carry):
@@ -50,12 +51,16 @@
     for other in (
         ctx_of((z + 1) % planes, y, core),
         ctx_of((z + planes - 1) % planes, y, core),
+        ctx_of((z + planes + 1 - 2 * core) % planes, y, 1 - core),
         ctx_of(z, y, 1 - core),
         ctx_of(z, y + 1 - 2 * (y % 2), 1 - core),
     ):
         pl.semaphore_signal(barrier, inc=1, device_id=(other, x), device_id_type=MESH)
     lax.fori_loop(1, PLANE, one, 0)
-    pl.semaphore_wait(barrier, PLANE + 3)
+
+
+def all_here():
+    pl.semaphore_wait(pltpu.get_barrier_semaphore(), PLANE + 4)
 
 
 def remote(src, dst, send, recv, ctx, x):
@@ -74,6 +79,7 @@
     qd_out,
     sel_out,
     store,
+    acc,
     q,
     g,
     k,
@@ -114,13 +120,14 @@
     ]
     for copy in loads:
         copy.start()
+    announce(planes, x, y, z, core)
     for copy in loads[:2]:
         copy.wait()
     for b in range(2):
         tokens = pl.ds(b * BLOCK, BLOCK)
         kv[:, b, 0] = jnp.swapaxes(k[tokens], 0, 1)
         kv[:, b, 1] = jnp.swapaxes(v[tokens], 0, 1)
-    greet(planes, x, y, z, core)
+    all_here()
 
     def near(d):
         to = (y + d) % SIDE
@@ -149,52 +156,79 @@
             sel, sel_all.at[x], i_send.at[d - 1], i_recv.at[d - 1], ctx_of(z, y, core), (x + d) % SIDE
         )
 
-    def at(d, j, side, first, count):
-        origin = (z + planes - j) % planes if d == 0 else (z + j) % planes
-        return store.at[pl.ds(origin * 16 + side * 8 + first, count)]
-
-    def piece(d, j, side, i, split):
-        first = 2 * piece_of(parity, i)
-        if split and i == 1:
-            return at(d, j, side, first + d, 1)
-        return at(d, j, side, first, 2)
-
-    def hop(d, s, i, split=False):
-        to = (z + 1) % planes if d == 0 else (z + planes - 1) % planes
-        part = piece(d, s - 1, core, i, split)
-        sems = ring_send.at[d, s - 1, i], ring_recv.at[d, s - 1, i]
-        return remote(part, part, *sems, ctx_of(to, y, core), x)
-
-    def arrived(d, s, i, split=False):
-        part = piece(d, s, core, i, split)
-        sems = ring_send.at[d, s - 1, i], ring_recv.at[d, s - 1, i]
-        return remote(part, part, *sems, ctx_of(z, y, 1 - core), x)
-
-    def share(d, s, i, side, split=False):
-        part = piece(d, s, side, i, split)
-        sems = pair_send.at[d, s - 1, i], pair_recv.at[d, s - 1, i]
-        return remote(part, part, *sems, ctx_of(z, y, 1 - core), x)
+    way = 1 - 2 * core
+    ahead = ctx_of((z + planes + way) % planes, y, core)
+    partner = ctx_of(z, y, 1 - core)
+
+    def piece(j, towards, side, row, count=2):
+        origin = (z + planes - j * towards) % planes
+        return store.at[pl.ds(origin * 16 + side * 8 + row, count)]
+
+    def here(j, k, i):
+        return piece(j, way, (core + k) % 2, 2 * piece_of(parity, i))
+
+    def there(j, k, i):
+        return piece(j, -way, (1 - core + k) % 2, 2 * piece_of(parity, i))
+
+    def left_out(j, k):
+        return piece(j, way, (core + k) % 2, 6 * (1 - parity))
+
+    def hop(s, k, i):
+        part = here(s - 1, k, i)
+        return remote(part, part, ring_send.at[s - 1, k, i], ring_recv.at[s - 1, k, i], ahead, x)
+
+    def arrived(j, k, i):
+        part = here(j, k, i)
+        return remote(part, part, ring_send.at[j - 1, k, i], ring_recv.at[j - 1, k, i], ahead, x)
+
+    def share(j, k, i):
+        part = here(j, k, i)
+        return remote(part, part, pair_send.at[j - 1, k, i], pair_recv.at[j - 1, k, i], partner, x)
+
+    def shared(j, k, i):
+        part = there(j, k, i)
+        return remote(part, part, pair_send.at[j - 1, k, i], pair_recv.at[j - 1, k, i], partner, x)
 
     def share_own(side):
-        part = at(0, 0, side, 0, 8)
-        sems = own_sem.at[1], own_sem.at[2]
-        return remote(part, part, *sems, ctx_of(z, y, 1 - core), x)
-
-    def cross(d, s, first):
-        part = at(d, s, core, 6 * first, 2)
-        sems = mate_send.at[d, s - 1], mate_recv.at[d, s - 1]
+        part = piece(0, 1, side, 0, 8)
+        return remote(part, part, own_sem.at[1], own_sem.at[2], partner, x)
+
+    def cross(j, k):
+        part = here(j, k, 0)
+        sems = mate_send.at[j - 1, k], mate_recv.at[j - 1, k]
         return remote(part, part, *sems, ctx_of(z, mate, core), x)
 
-    def over(d, s, side):
-        part = at(d, s, side, 6 * (1 - parity), 2)
-        sems = over_send.at[d, s - 1], over_recv.at[d, s - 1]
-        return remote(part, part, *sems, ctx_of(z, y, 1 - core), x)
-
-    def cross_over(first, side):
-        part = at(0, half_way, side, 6 * first, 2)
-        sems = over_send.at[0, last], over_recv.at[0, last]
+    def crossed(j, k):
+        part = left_out(j, k)
+        sems = mate_send.at[j - 1, k], mate_recv.at[j - 1, k]
+        return remote(part, part, *sems, ctx_of(z, mate, core), x)
+
+    def over(j, k):
+        part = left_out(j, k)
+        return remote(part, part, over_send.at[j - 1, k], over_recv.at[j - 1, k], partner, x)
+
+    def overed(j, k):
+        part = piece(j, -way, (1 - core + k) % 2, 6 * (1 - parity))
+        return remote(part, part, over_send.at[j - 1, k], over_recv.at[j - 1, k], partner, x)
+
+    def cross_over(row, side):
+        part = piece(half_way, 1, side, row)
+        sems = over_send.at[last, 0], over_recv.at[last, 0]
         return remote(part, part, *sems, ctx_of(z, mate, 1 - core), x)
 
+    def first(i, row):
+        part = piece(0, 1, core, row)
+        return remote(part, part, ring_send.at[0, 0, i], ring_recv.at[0, 0, i], ahead, x)
+
+    outer = 2 * (((y + 1) // 2) % 2)
+    remote(
+        kv.at[2 * x + y // 2],
+        piece(0, 1, core, 2 * y),
+        ring_send.at[0, 0, outer],
+        ring_recv.at[0, 0, outer],
+        ahead,
+        x,
+    ).start()
     for d in range(1, SIDE):
         near(d).start()
     mine = pltpu.make_async_copy(
@@ -213,9 +247,8 @@
     mine.wait()
     for d in range(1, SIDE):
         near(d).wait_recv()
-    for i in range(3):
-        for d in range(2):
-            hop(d, 1, i).start()
+    first(2 - outer, 2 * (2 * parity + 2 - y)).start()
+    first(1, 2 * (parity + 1)).start()
     share_own(core).start()
 
     def send_query(i, carry):
@@ -225,47 +258,54 @@
     lax.fori_loop(1, PLANE, send_query, 0)
     qd_out[x * SIDE + y] = qd[unit_of(x, y)]
     sel_all[x] = sel[...]
+    share_own(1 - core).wait_recv()
+    for i in range(3):
+        hop(1, 1, i).start()
+
+    def clear(i, carry):
+        acc[pl.ds(i * 4, 4)] = jnp.zeros((4, 2, BLOCK, HEAD), jnp.bfloat16)
+        return carry
+
+    lax.fori_loop(0, acc.shape[0] // 4, clear, 0)
 
     def step(s, carry):
-        for i in range(3):
-            for d in range(2):
-                arrived(d, s - 1, i).wait_recv()
-                hop(d, s, i).start()
+        for k in range(2):
+            for i in range(3):
+                arrived(s - 1, k, i).wait_recv()
+                hop(s, k, i).start()
                 if i == 0:
-                    cross(d, s - 1, parity).start()
-                share(d, s - 1, i, core).start()
+                    cross(s - 1, k).start()
+                share(s - 1, k, i).start()
 
         @pl.when(s > 2)
         def _():
-            for d in range(2):
-                cross(d, s - 2, 1 - parity).wait_recv()
-                over(d, s - 2, core).start()
+            for k in range(2):
+                crossed(s - 2, k).wait_recv()
+                over(s - 2, k).start()
 
         return carry
 
     lax.fori_loop(2, half_way, step, 0)
+    for k in range(2):
+        for i in range(3):
+            arrived(last, k, i).wait_recv()
+            if k == 0:
+                hop(half_way, 0, i).start()
+            if i == 0:
+                cross(last, k).start()
+            share(last, k, i).start()
+    for k in range(2):
+        crossed(last - 1, k).wait_recv()
+        over(last - 1, k).start()
     for i in range(3):
-        for d in range(2):
-            arrived(d, last, i).wait_recv()
-            if i in HALVES[d]:
-                hop(d, half_way, i, True).start()
-            if i == 0:
-                cross(d, last, parity).start()
-            share(d, last, i, core).start()
-    for d in range(2):
-        cross(d, last - 1, 1 - parity).wait_recv()
-        over(d, last - 1, core).start()
+        arrived(half_way, 0, i).wait_recv()
+        if i == 0:
+            cross(half_way, 0).start()
+            cross_over(6 * parity, core).start()
+        share(half_way, 0, i).start()
     for k in range(2):
-        for d in range(2):
-            i = HALVES[d][k]
-            arrived(d, half_way, i, True).wait_recv()
-            if i == 0:
-                cross(0, half_way, parity).start()
-                cross_over(parity, core).start()
-            share(d, half_way, i, core, True).start()
-    for d in range(2):
-        cross(d, last, 1 - parity).wait_recv()
-        over(d, last, core).start()
+        crossed(last, k).wait_recv()
+        over(last, k).start()
 
     def finish_query(i, carry):
         query(i).wait()
@@ -280,47 +320,50 @@
 
     for d in range(1, SIDE):
         near(d).wait_send()
-    share_own(1 - core).wait_recv()
     share_own(core).wait_send()
-
-    def finish(s, carry):
-        for d in range(2):
+    for i in range(3):
+        hop(1, 0, i).wait_send()
+        hop(1, 1, i).wait_send()
+
+    def finish(j, carry):
+        for k in range(2):
             for i in range(3):
-                hop(d, s, i).wait_send()
-                share(d, s, i, 1 - core).wait_recv()
-                share(d, s, i, core).wait_send()
-            cross(d, s, parity).wait_send()
-            over(d, s, 1 - core).wait_recv()
-            over(d, s, core).wait_send()
+                shared(j, k, i).wait_recv()
+                share(j, k, i).wait_send()
+            cross(j, k).wait_send()
+            overed(j, k).wait_recv()
+            over(j, k).wait_send()
         return carry
 
     lax.fori_loop(1, half_way, finish, 0)
-    for d in range(2):
-        for i in HALVES[d]:
-            hop(d, half_way, i, True).wait_send()
-            share(d, half_way, i, 1 - core, True).wait_recv()
-            share(d, half_way, i, core, True).wait_send()
-    cross(0, half_way, parity).wait_send()
-    cross_over(parity, core).wait_send()
-    cross(0, half_way, 1 - parity).wait_recv()
-    cross_over(1 - parity, 1 - core).wait_recv()
-
-
-def attend(sel, qd, store, od, acc):
+
+    def finish_hop(s, carry):
+        for k in range(2):
+            for i in range(3):
+                hop(s, k, i).wait_send()
+        return carry
+
+    lax.fori_loop(2, half_way, finish_hop, 0)
+    for i in range(3):
+        hop(half_way, 0, i).wait_send()
+        shared(half_way, 0, i).wait_recv()
+        share(half_way, 0, i).wait_send()
+    cross(half_way, 0).wait_send()
+    cross_over(6 * parity, core).wait_send()
+    crossed(half_way, 0).wait_recv()
+    cross_over(6 * (1 - parity), 1 - core).wait_recv()
+
+
+def attend(sel, qd, store, cleared, od, acc):
     x, y, z, core = place()
     parity = y % 2
     factor = HEAD**-0.5
+    rate = factor * math.log2(math.e)
     f32, bf16 = jnp.float32, jnp.bfloat16
     nt = (((1,), (1,)), ((), ()))
     nn = (((1,), (0,)), ((), ()))
     tn = (((0,), (0,)), ((), ()))
 
-    def clear(i, carry):
-        acc[pl.ds(i * 4, 4)] = jnp.zeros((4, 2, BLOCK, HEAD), bf16)
-        return carry
-
-    lax.fori_loop(0, acc.shape[0] // 4, clear, 0)
-
     def dot(a, b, dims):
         return lax.dot_general(a, b, dims, preferred_element_type=f32)
 
@@ -328,33 +371,50 @@
         own = z * 16 + core * 8 + side * 2 + parity
         block = ((z * SIDE + side) * 2 + core) * 2 + parity
         own_terms = [jnp.zeros((BLOCK, HEAD), f32)] * 2
-        for group in range(SIDE):
-            u = group * SIDE + side
-            rows = [own]
+        groups = range(SIDE)
+        rows, keys, values = {}, {}, {}
+        for group in groups:
+            rows[group] = [own]
             for t in range(3):
                 n = sel[group, t, block]
-                rows.append((n // 16) * 16 + ((n // 2) % 2) * 8 + ((n // 4) % SIDE) * 2 + n % 2)
-            q = qd[u, 0]
-            g = qd[u, 1]
-            keys = jnp.concatenate([store[r, 0] for r in rows], axis=0)
-            values = jnp.concatenate([store[r, 1] for r in rows], axis=0)
-            scores = dot(q, keys, nt) * factor
-            top = jnp.max(scores, axis=1, keepdims=True)
-            e = jnp.exp(scores - top)
-            prob = e * (1.0 / jnp.sum(e, axis=1, keepdims=True))
-            prob_b = prob.astype(bf16)
-            out = dot(prob_b, values, nn).astype(bf16)
-            od[u, 0] = out
-            delta = jnp.sum(g.astype(f32) * out.astype(f32), axis=1, keepdims=True)
-            grad_prob = dot(g, values, nt)
-            grad_scores = (prob * (grad_prob - delta)).astype(bf16)
-            od[u, 1] = (dot(grad_scores, keys, nn) * factor).astype(bf16)
-            terms = dot(grad_scores, q, tn) * factor, dot(prob_b, g, tn)
-            for i in range(2):
-                own_terms[i] += terms[i][:BLOCK]
+                rows[group].append(
+                    (n // 16) * 16 + ((n // 2) % 2) * 8 + ((n // 4) % SIDE) * 2 + n % 2
+                )
+        for group in groups:
+            keys[group] = jnp.concatenate([store[r, 0] for r in rows[group]], axis=0)
+            values[group] = jnp.concatenate([store[r, 1] for r in rows[group]], axis=0)
+        q = {group: qd[group * SIDE + side, 0] for group in groups}
+        g = {group: qd[group * SIDE + side, 1] for group in groups}
+        scores = {group: dot(q[group], keys[group], nt) for group in groups}
+        grad_prob = {group: dot(g[group], values[group], nt) for group in groups}
+        top = {group: jnp.max(scores[group], axis=1, keepdims=True) for group in groups}
+        e = {group: jnp.exp2((scores[group] - top[group]) * rate) for group in groups}
+        total = {group: jnp.sum(e[group], axis=1, keepdims=True) for group in groups}
+        inverse = {group: 1.0 / total[group] for group in groups}
+        prob_b = {group: (e[group] * inverse[group]).astype(bf16) for group in groups}
+        scaled = {group: e[group] * (inverse[group] * factor) for group in groups}
+        out = {group: dot(prob_b[group], values[group], nn).astype(bf16) for group in groups}
+        value_terms = {group: dot(prob_b[group], g[group], tn) for group in groups}
+        delta = {
+            group: jnp.sum(g[group].astype(f32) * out[group].astype(f32), axis=1, keepdims=True)
+            for group in groups
+        }
+        grad_scores = {
+            group: (scaled[group] * (grad_prob[group] - delta[group])).astype(bf16)
+            for group in groups
+        }
+        key_terms = {group: dot(grad_scores[group], q[group], tn) for group in groups}
+        query_terms = {group: dot(grad_scores[group], keys[group], nn) for group in groups}
+        for group in groups:
+            u = group * SIDE + side
+            od[u, 0] = out[group]
+            od[u, 1] = query_terms[group].astype(bf16)
+            for i, terms in enumerate((key_terms[group], value_terms[group])):
+                own_terms[i] += terms[:BLOCK]
                 for t in range(1, 4):
-                    part = terms[i][t * BLOCK : (t + 1) * BLOCK]
-                    acc[rows[t], i] = (acc[rows[t], i].astype(f32) + part).astype(bf16)
+                    row = rows[group][t]
+                    part = terms[t * BLOCK : (t + 1) * BLOCK]
+                    acc[row, i] = (acc[row, i].astype(f32) + part).astype(bf16)
         for i in range(2):
             acc[own, i] = (acc[own, i].astype(f32) + own_terms[i]).astype(bf16)
         return carry
@@ -396,9 +456,10 @@
     heads = att.shape[1]
     f32, bf16 = jnp.float32, jnp.bfloat16
 
+    announce(planes, x, y, z, core)
     for d in range(2):
         inbox[d, 0, 1, 1 - d] = jnp.zeros((2, BLOCK, HEAD), bf16)
-    greet(planes, x, y, z, core)
+    all_here()
 
     def chunk(d, s):
         far = half_way - s
@@ -527,6 +588,16 @@
 
     lax.fori_loop(2, half_way, step, 0)
 
+    def scatter(to):
+        @pl.when(to != y)
+        def _():
+            near((to + SIDE - y) % SIDE).start()
+
+    pair(z).wait_recv()
+    rest = 6 * (1 - parity)
+    fin[pl.ds(rest, 2)] = chip_sum(z, rest, 2).astype(bf16)
+    scatter(3 * (1 - parity))
+
     def finish_answer(i, carry):
         answer(i).wait()
         return carry
@@ -539,9 +610,6 @@
         att[tokens] = jnp.swapaxes(od_all[units, 0], 0, 1)
         grad_q[tokens] = jnp.swapaxes(od_all[units, 1], 0, 1)
 
-    pair(z).wait_recv()
-    rest = 6 * (1 - parity)
-    fin[pl.ds(rest, 2)] = chip_sum(z, rest, 2).astype(bf16)
     for i in (2, 1, 0):
         first = 2 * piece_of(parity, i)
         total = chip_sum(z, first, 2)
@@ -549,8 +617,7 @@
             hop(d, half_way - 1, i).wait_recv()
             total += inbox[d, half_way - 1, i].astype(f32)
         fin[pl.ds(first, 2)] = total.astype(bf16)
-    for d in range(1, SIDE):
-        near(d).start()
+        scatter(piece_of(parity, i))
     spread[y] = fin[pl.ds(y * 2, 2)]
 
     def finish(s, carry):
@@ -611,12 +678,17 @@
     lists = (3, heads, blocks)
     given = queries, grad_out, key_states, value_states, selected.transpose(2, 1, 0)
 
-    qd, sel, store = pl.pallas_call(
+    qd, sel, store, cleared = pl.pallas_call(
         functools.partial(bring, planes),
         name="bring",
-        out_shape=(shape(units, bf16), shape((SIDE, 3, blocks), jnp.int32), shape(rows, bf16)),
+        out_shape=(
+            shape(units, bf16),
+            shape((SIDE, 3, blocks), jnp.int32),
+            shape(rows, bf16),
+            shape(rows, bf16),
+        ),
         in_specs=[HBM] * 5,
-        out_specs=(VMEM,) * 3,
+        out_specs=(VMEM,) * 4,
         scratch_shapes=[
             pltpu.VMEM(queries.shape, bf16),
             pltpu.VMEM(queries.shape, bf16),
@@ -633,14 +705,14 @@
             dma((PLANE - 1,)),
             dma((SIDE - 1,)),
             dma((SIDE - 1,)),
-            dma((2, half_way, 3)),
-            dma((2, half_way, 3)),
-            dma((2, half_way, 3)),
-            dma((2, half_way, 3)),
-            dma((2, half_way)),
-            dma((2, half_way)),
-            dma((2, half_way)),
-            dma((2, half_way)),
+            dma((half_way, 2, 3)),
+            dma((half_way, 2, 3)),
+            dma((half_way, 2, 3)),
+            dma((half_way, 2, 3)),
+            dma((half_way, 2)),
+            dma((half_way, 2)),
+            dma((half_way, 2)),
+            dma((half_way, 2)),
             dma((3,)),
         ],
         compiler_params=pltpu.CompilerParams(
@@ -652,10 +724,11 @@
         attend,
         name="attend",
         out_shape=(shape(units, bf16), shape(rows, bf16)),
-        in_specs=[SMEM, VMEM, VMEM],
+        in_specs=[SMEM, VMEM, VMEM, VMEM],
         out_specs=(VMEM, VMEM),
+        input_output_aliases={3: 1},
         compiler_params=pltpu.CompilerParams(vmem_limit_bytes=24 * 1024 * 1024),
-    )(sel, qd, store)
+    )(sel, qd, store, cleared)
 
     piece = (3, 2, 2, BLOCK, HEAD)
     att, grad_q, kvg = pl.pallas_call(

time: 124 us -> 114 us (0.919)
  Pallas kernels: 123 us -> 114 us
    pallas_call x1, Pallas kernels: 12.6 us -> 5.43 us  [local(): pl.pallas_call(attend, name='attend', out_shape=(shape(units, bf16), shap...]
    pallas_call x1, Pallas kernels: 57.1 us -> 55.3 us  [local(): pl.pallas_call(functools.partial(bring, planes), name='bring', out_shape=...]
where the time goes in v3:
time: 114 us
  Pallas kernels  114 us (100%)
    pallas_call x1, Pallas kernels, local(): pl.pallas_call(functools.partial(bring, planes), name='bring', out_shape=...  55.3 us
    pallas_call x1, Pallas kernels, local(): pl.pallas_call(functools.partial(give, planes), name='give', out_shape=(s...  52 us
    pallas_call x1, Pallas kernels, local(): pl.pallas_call(attend, name='attend', out_shape=(shape(units, bf16), shap...  5.43 us

profile of v3, /device:TPU:6, one launch (start us, length us, event | category | flops | bytes accessed | tf_op | source)
XLA Modules:
  0.0 114.2 jit_solution(4906147085674522453)
XLA Ops:
  0.6 55.3 %bring.1 = (bf16[16,2,64,128]{3,2,1,0:T(8,128)(2,1)S(1)}, s32[4,3,256]{2,1,0:T(4,128)S(1)}, bf16[256,2,64,128]{3,2,1,0:T(8,128)(2,1)S(1)}, bf16[256,2,64,128]{3,2,1,0:T(8,128)(2,1)S(1)}) custom-call(bf16[128,8,128]{2,1,0:T(8,128)(2,1)} %q_hbm.1, bf16[128,8,128]{2,1,0:T(8,128)(2,1)} %g_hbm.1, bf16[128,8,128]{2,1,0:T(8,128)(2,1)} %k_hbm.1, ...), custom_call_target="tpu_custom_call" | custom-call | tf_op jit(solution)/shard_map/bring/pallas_call | solution.py:681
  55.9 5.4 %attend.1 = (bf16[16,2,64,128]{3,2,1,0:T(8,128)(2,1)S(1)}, bf16[256,2,64,128]{3,2,1,0:T(8,128)(2,1)S(1)}) custom-call(s32[4,3,256]{2,1,0:T(4,128)S(1)} %get-tuple-element.13.sel, bf16[16,2,64,128]{3,2,1,0:T(8,128)(2,1)S(1)} %get-tuple-element.14.qd, bf16[256,2,64,128]{3,2,1,0:T(8,128)(2,1)S(1)} %get-tuple-element.15.store, ...), custom_call_target="tpu_custom_call", output_to_operand_aliasing={{1}: (3, {})} | custom-call | tf_op jit(solution)/shard_map/attend/pallas_call | solution.py:723
  61.4 52.0 %give.1 = (bf16[128,8,128]{2,1,0:T(8,128)(2,1)S(1)}, bf16[128,8,128]{2,1,0:T(8,128)(2,1)S(1)}, bf16[2,2,2,64,128]{4,3,2,1,0:T(8,128)(2,1)S(1)}) custom-call(bf16[16,2,64,128]{3,2,1,0:T(8,128)(2,1)S(1)} %get-tuple-element.17.od, bf16[256,2,64,128]{3,2,1,0:T(8,128)(2,1)S(1)} %get-tuple-element.18.acc), custom_call_target="tpu_custom_call" | custom-call | tf_op jit(solution)/shard_map/give/pallas_call | solution.py:734
  113.3 0.9 leave.1

commit v4 on v3

--- a/solution.py
+++ b/solution.py
@@ -268,6 +268,16 @@
 
     lax.fori_loop(0, acc.shape[0] // 4, clear, 0)
 
+    def retire(j):
+        for k in range(2):
+            for i in range(3):
+                hop(j, k, i).wait_send()
+                shared(j, k, i).wait_recv()
+                share(j, k, i).wait_send()
+            cross(j, k).wait_send()
+            overed(j, k).wait_recv()
+            over(j, k).wait_send()
+
     def step(s, carry):
         for k in range(2):
             for i in range(3):
@@ -283,9 +293,27 @@
                 crossed(s - 2, k).wait_recv()
                 over(s - 2, k).start()
 
+        @pl.when(s > 4)
+        def _():
+            retire(s - 4)
+
         return carry
 
     lax.fori_loop(2, half_way, step, 0)
+    def finish_query(i, carry):
+        query(i).wait()
+        return carry
+
+    lax.fori_loop(1, PLANE, finish_query, 0)
+    for d in range(1, SIDE):
+        index(d).wait()
+    own_head = lax.broadcasted_iota(jnp.int32, sel.shape, 1) == 2 * x + y // 2
+    for group in range(SIDE):
+        sel_out[group] = jnp.sum(jnp.where(own_head, sel_all[group], 0), axis=1)
+    for d in range(1, SIDE):
+        near(d).wait_send()
+    share_own(core).wait_send()
+    retire(last - 3)
     for k in range(2):
         for i in range(3):
             arrived(last, k, i).wait_recv()
@@ -297,6 +325,7 @@
     for k in range(2):
         crossed(last - 1, k).wait_recv()
         over(last - 1, k).start()
+    retire(last - 2)
     for i in range(3):
         arrived(half_way, 0, i).wait_recv()
         if i == 0:
@@ -307,43 +336,8 @@
         crossed(last, k).wait_recv()
         over(last, k).start()
 
-    def finish_query(i, carry):
-        query(i).wait()
-        return carry
-
-    lax.fori_loop(1, PLANE, finish_query, 0)
-    for d in range(1, SIDE):
-        index(d).wait()
-    own_head = lax.broadcasted_iota(jnp.int32, sel.shape, 1) == 2 * x + y // 2
-    for group in range(SIDE):
-        sel_out[group] = jnp.sum(jnp.where(own_head, sel_all[group], 0), axis=1)
-
-    for d in range(1, SIDE):
-        near(d).wait_send()
-    share_own(core).wait_send()
-    for i in range(3):
-        hop(1, 0, i).wait_send()
-        hop(1, 1, i).wait_send()
-
-    def finish(j, carry):
-        for k in range(2):
-            for i in range(3):
-                shared(j, k, i).wait_recv()
-                share(j, k, i).wait_send()
-            cross(j, k).wait_send()
-            overed(j, k).wait_recv()
-            over(j, k).wait_send()
-        return carry
-
-    lax.fori_loop(1, half_way, finish, 0)
-
-    def finish_hop(s, carry):
-        for k in range(2):
-            for i in range(3):
-                hop(s, k, i).wait_send()
-        return carry
-
-    lax.fori_loop(2, half_way, finish_hop, 0)
+    retire(last - 1)
+    retire(last)
     for i in range(3):
         hop(half_way, 0, i).wait_send()
         shared(half_way, 0, i).wait_recv()
@@ -552,10 +546,6 @@
     home = pltpu.make_async_copy(od.at[x * SIDE + y], od_all.at[unit_of(x, y)], mine_sem)
     home.start()
 
-    def send_answer(i, carry):
-        answer(i).start()
-        return carry
-
     prepare(chunk(0, 0))
     for d in range(2):
         emit(d, 0, 1, False)
@@ -564,7 +554,6 @@
         prepare(chunk(d, 1))
     cross(chunk(0, 0)).wait_recv()
     emit(0, 0, 0, False)
-    lax.fori_loop(1, PLANE, send_answer, 0)
     for d in range(2):
         prepare(chunk(d, 2))
     for i in (2, 1, 0):
@@ -573,11 +562,15 @@
                 cross(chunk(d, 1)).wait_recv()
             emit(d, 1, i, i in HALVES[d])
 
+    each = (PLANE - 1) // (half_way - 3)
+
     def step(s, carry):
         @pl.when(s + 1 < half_way)
         def _():
             for d in range(2):
                 prepare(chunk(d, s + 1))
+            for i in range(1, 1 + each):
+                answer((s - 2) * each + i).start()
 
         for i in (2, 1, 0):
             for d in range(2):

time: 114 us -> 112 us (0.982)
  Pallas kernels: 114 us -> 111 us
    pallas_call x1, Pallas kernels: 52 us -> 49.8 us  [local(): pl.pallas_call(functools.partial(give, planes), name='give', out_shape=(s...]
where the time goes in v4:
time: 112 us
  Pallas kernels  111 us (99%)
    pallas_call x1, Pallas kernels, local(): pl.pallas_call(functools.partial(bring, planes), name='bring', out_shape=...  55.3 us
    pallas_call x1, Pallas kernels, local(): pl.pallas_call(functools.partial(give, planes), name='give', out_shape=(s...  49.8 us
    pallas_call x1, Pallas kernels, local(): pl.pallas_call(attend, name='attend', out_shape=(shape(units, bf16), shap...  5.43 us

profile of v4, /device:TPU:6, one launch (start us, length us, event | category | flops | bytes accessed | tf_op | source)
XLA Modules:
  0.0 112.0 jit_solution(13381570350930626113)
XLA Ops:
  0.6 55.3 %bring.1 = (bf16[16,2,64,128]{3,2,1,0:T(8,128)(2,1)S(1)}, s32[4,3,256]{2,1,0:T(4,128)S(1)}, bf16[256,2,64,128]{3,2,1,0:T(8,128)(2,1)S(1)}, bf16[256,2,64,128]{3,2,1,0:T(8,128)(2,1)S(1)}) custom-call(bf16[128,8,128]{2,1,0:T(8,128)(2,1)} %q_hbm.1, bf16[128,8,128]{2,1,0:T(8,128)(2,1)} %g_hbm.1, bf16[128,8,128]{2,1,0:T(8,128)(2,1)} %k_hbm.1, ...), custom_call_target="tpu_custom_call" | custom-call | tf_op jit(solution)/shard_map/bring/pallas_call | solution.py:674
  55.9 5.4 %attend.1 = (bf16[16,2,64,128]{3,2,1,0:T(8,128)(2,1)S(1)}, bf16[256,2,64,128]{3,2,1,0:T(8,128)(2,1)S(1)}) custom-call(s32[4,3,256]{2,1,0:T(4,128)S(1)} %get-tuple-element.13.sel, bf16[16,2,64,128]{3,2,1,0:T(8,128)(2,1)S(1)} %get-tuple-element.14.qd, bf16[256,2,64,128]{3,2,1,0:T(8,128)(2,1)S(1)} %get-tuple-element.15.store, ...), custom_call_target="tpu_custom_call", output_to_operand_aliasing={{1}: (3, {})} | custom-call | tf_op jit(solution)/shard_map/attend/pallas_call | solution.py:716
  61.3 49.8 %give.1 = (bf16[128,8,128]{2,1,0:T(8,128)(2,1)S(1)}, bf16[128,8,128]{2,1,0:T(8,128)(2,1)S(1)}, bf16[2,2,2,64,128]{4,3,2,1,0:T(8,128)(2,1)S(1)}) custom-call(bf16[16,2,64,128]{3,2,1,0:T(8,128)(2,1)S(1)} %get-tuple-element.17.od, bf16[256,2,64,128]{3,2,1,0:T(8,128)(2,1)S(1)} %get-tuple-element.18.acc), custom_call_target="tpu_custom_call" | custom-call | tf_op jit(solution)/shard_map/give/pallas_call | solution.py:727
  111.1 0.9 leave.1

commit v5 on v4

--- a/solution.py
+++ b/solution.py
@@ -540,16 +540,16 @@
         pair(chunk(1, s)).start()
         return carry
 
-    lax.fori_loop(1, half_way, begin_step, 0)
-    pair(z).start()
-
-    home = pltpu.make_async_copy(od.at[x * SIDE + y], od_all.at[unit_of(x, y)], mine_sem)
-    home.start()
+    begin_step(1, 0)
 
     prepare(chunk(0, 0))
     for d in range(2):
         emit(d, 0, 1, False)
     emit(1, 0, 2, False)
+    lax.fori_loop(2, half_way, begin_step, 0)
+    pair(z).start()
+    home = pltpu.make_async_copy(od.at[x * SIDE + y], od_all.at[unit_of(x, y)], mine_sem)
+    home.start()
     for d in range(2):
         prepare(chunk(d, 1))
     cross(chunk(0, 0)).wait_recv()

time: 112 us -> 112 us (level)
  no operation moved by 1% of the time
where the time goes in v5:
time: 112 us
  Pallas kernels  111 us (99%)
    pallas_call x1, Pallas kernels, local(): pl.pallas_call(functools.partial(bring, planes), name='bring', out_shape=...  55.3 us
    pallas_call x1, Pallas kernels, local(): pl.pallas_call(functools.partial(give, planes), name='give', out_shape=(s...  49.8 us
    pallas_call x1, Pallas kernels, local(): pl.pallas_call(attend, name='attend', out_shape=(shape(units, bf16), shap...  5.43 us

profile of v5, /device:TPU:6, one launch (start us, length us, event | category | flops | bytes accessed | tf_op | source)
XLA Modules:
  0.0 112.0 jit_solution(8529825385143124845)
XLA Ops:
  0.6 55.3 %bring.1 = (bf16[16,2,64,128]{3,2,1,0:T(8,128)(2,1)S(1)}, s32[4,3,256]{2,1,0:T(4,128)S(1)}, bf16[256,2,64,128]{3,2,1,0:T(8,128)(2,1)S(1)}, bf16[256,2,64,128]{3,2,1,0:T(8,128)(2,1)S(1)}) custom-call(bf16[128,8,128]{2,1,0:T(8,128)(2,1)} %q_hbm.1, bf16[128,8,128]{2,1,0:T(8,128)(2,1)} %g_hbm.1, bf16[128,8,128]{2,1,0:T(8,128)(2,1)} %k_hbm.1, ...), custom_call_target="tpu_custom_call" | custom-call | tf_op jit(solution)/shard_map/bring/pallas_call | solution.py:674
  55.9 5.4 %attend.1 = (bf16[16,2,64,128]{3,2,1,0:T(8,128)(2,1)S(1)}, bf16[256,2,64,128]{3,2,1,0:T(8,128)(2,1)S(1)}) custom-call(s32[4,3,256]{2,1,0:T(4,128)S(1)} %get-tuple-element.13.sel, bf16[16,2,64,128]{3,2,1,0:T(8,128)(2,1)S(1)} %get-tuple-element.14.qd, bf16[256,2,64,128]{3,2,1,0:T(8,128)(2,1)S(1)} %get-tuple-element.15.store, ...), custom_call_target="tpu_custom_call", output_to_operand_aliasing={{1}: (3, {})} | custom-call | tf_op jit(solution)/shard_map/attend/pallas_call | solution.py:716
  61.3 49.8 %give.1 = (bf16[128,8,128]{2,1,0:T(8,128)(2,1)S(1)}, bf16[128,8,128]{2,1,0:T(8,128)(2,1)S(1)}, bf16[2,2,2,64,128]{4,3,2,1,0:T(8,128)(2,1)S(1)}) custom-call(bf16[16,2,64,128]{3,2,1,0:T(8,128)(2,1)S(1)} %get-tuple-element.17.od, bf16[256,2,64,128]{3,2,1,0:T(8,128)(2,1)S(1)} %get-tuple-element.18.acc), custom_call_target="tpu_custom_call" | custom-call | tf_op jit(solution)/shard_map/give/pallas_call | solution.py:727
  111.1 0.9 leave.1
